TPU v7x, 128 devices: a whole 4x4x4 slice. The times are simulated.
128 devices in a mesh: row: 16 (over x, y), col: 8 (over z, core).
Axes of the slice: x: 4, y: 4, z: 4, core: 2. Of those that a mesh axis runs over, the one named last changes fastest.
Arguments:
- saved_factor: float32 [8192, 8192], P('row', 'col'), may hold values from -1 to 3, as said below
- cotangent: float32 [8192, 8192], P('row', 'col'), may hold values from -6 to 6
Outputs:
- adjoint: float32 [8192, 8192], P('row', 'col')
Inputs may be any that keep to these rules, and one draw needn't show every extreme that they name: `saved_factor`: entry (i, j) is zero where j > i + 8192 - 3 * 512, and 1 or more where j = i + 8192 - 3 * 512.
All inputs are finite; a program needn't handle non-finite values.
Results may differ from a plain program's by a relative error of at most 0.0001.
Values sent between devices are 32-bit elements; how exact they have to be, the bound alone decides.
A program may use at most 128 MiB of HBM per device.

v0:
```python
import jax
import jax.numpy as jnp
from jax import lax
from jax.experimental import pallas as pl
from jax.experimental.pallas import tpu as pltpu
from jax.sharding import PartitionSpec as P

NB = 512
NP = 3
MESH = pl.DeviceIdType.MESH
HI = lax.Precision.HIGHEST
MID = lax.Precision.HIGH
F32 = jnp.float32


def dot(a, b, precision=MID):
    return jnp.dot(a, b, precision=precision, preferred_element_type=F32)


def dot_t(a, b, precision=MID):
    return lax.dot_general(
        a, b, (((0,), (0,)), ((), ())), precision=precision, preferred_element_type=F32
    )


def place():
    row = lax.axis_index("row")
    col = lax.axis_index("col")
    return row // 4, row % 4, col // 2, col % 2


def remote(src, dst, send, recv, x, y, z, core):
    return pltpu.make_async_remote_copy(
        src_ref=src,
        dst_ref=dst,
        send_sem=send,
        recv_sem=recv,
        device_id=(x * 4 + y, z * 2 + core),
        device_id_type=MESH,
    )


def greet(devices):
    barrier = pltpu.get_barrier_semaphore()
    for x, y, z, core in devices:
        pl.semaphore_signal(
            barrier, inc=1, device_id=(x * 4 + y, z * 2 + core), device_id_type=MESH
        )
    pl.semaphore_wait(barrier, len(devices))


def plane_and_peer(x, y, z, core):
    out = []
    for dx in range(4):
        for dy in range(4):
            if dx or dy:
                out.append(((x + dx) % 4, (y + dy) % 4, z, core))
    return out + [(x, y, z, 1 - core)]


CH = 8
CR = 128 // CH
LEFT, RIGHT = pl.ds(0, NB), pl.ds(NB, NB)
ROWS = (pl.ds(0, 16), pl.ds(16, 16))
PAIR = (pl.ds(0, 2), pl.ds(2, 2))


def unit(part, u, core):
    if part == 0:
        p = u + core if u < 2 else 2
        off = NB * (1 - core) if u < 2 else NB
    else:
        p = u - core if u >= 1 else 0
        off = NB * core if u >= 1 else 0
    if isinstance(off, int):
        return p, pl.ds(off, NB)
    return p, pl.ds(pl.multiple_of(off, NB), NB)


def line(order, x, y, d):
    return ((x + d) % 4, y) if order == 0 else (x, (y + d) % 4)


def spread_steps(part, own, strips, sems):
    scat_s, scat_r, one_s, one_r, two_s, two_r, loc = sems
    x, y, z, core = place()
    units = [unit(part, u, core) for u in range(NP)]

    def piece(ref, u, px, py):
        p, cols = units[u]
        if ref is own:
            return own.at[px, py, :, cols]
        return strips.at[p, px, py, :, cols]

    def scatter(u, d):
        tx, ty = (x + d // 4) % 4, (y + d % 4) % 4
        return remote(
            piece(own, u, tx, ty), piece(strips, u, tx, ty),
            scat_s.at[u, d], scat_r.at[u], tx, ty, z, core,
        )

    def keep(u):
        return pltpu.make_async_copy(piece(own, u, x, y), piece(strips, u, x, y), loc.at[u])

    roots = [(x == 0) & (y == units[u][0]) for u in range(NP)]
    for u in range(NP):

        @pl.when(roots[u])
        def _():
            keep(u).start()
            for d in range(15, 0, -1):
                scatter(u, d).start()

    yield

    for u in range(NP):

        @pl.when(roots[u])
        def _():
            keep(u).wait()

        @pl.when(jnp.logical_not(roots[u]))
        def _():
            here = piece(strips, u, x, y)
            remote(here, here, scat_s.at[u, 0], scat_r.at[u], x, y, z, 1 - core).wait_recv()

    first = []
    for u in range(NP):
        p, cols = units[u]
        for order in range(2):
            for d in range(1, 4):
                here = strips.at[p, x, y, ROWS[order], cols]
                tx, ty = line(order, x, y, d)
                first.append(
                    remote(
                        here, here, one_s.at[order, u, d], one_r.at[order, u, d],
                        tx, ty, z, core,
                    )
                )
    for copy in first:
        copy.start()
    yield

    for copy in first:
        copy.wait_recv()

    def block(order, u, at, pick):
        p, cols = units[u]
        if order == 0:
            return strips.at[p, pick, (y + at) % 4, ROWS[0], cols]
        return strips.at[p, (x + at) % 4, pick, ROWS[1], cols]

    def second(order, u, kind):
        whole = pl.ds(0, 4)
        at, pick, d = (
            (0, whole, 1), (0, whole, 3), (3, PAIR[0], 1), (1, PAIR[1], 3)
        )[kind]
        ref = block(order, u, at, pick)
        tx, ty = line(1 - order, x, y, d)
        return remote(
            ref, ref, two_s.at[order, u, kind], two_r.at[order, u, kind], tx, ty, z, core
        )

    def arrival(order, u, kind):
        whole = pl.ds(0, 4)
        at, pick = ((3, whole), (1, whole), (2, PAIR[0]), (2, PAIR[1]))[kind]
        ref = block(order, u, at, pick)
        return remote(
            ref, ref, two_s.at[order, u, kind], two_r.at[order, u, kind], x, y, z, 1 - core
        )

    every = [(order, u) for u in range(NP) for order in range(2)]
    for order, u in every:
        for kind in (0, 1):
            second(order, u, kind).start()
    yield

    for order, u in every:
        for kind in (0, 1):
            arrival(order, u, kind).wait_recv()
            second(order, u, kind + 2).start()
    yield

    for order, u in every:
        for kind in (2, 3):
            arrival(order, u, kind).wait_recv()
    yield

    for u in range(NP):

        @pl.when(roots[u])
        def _():
            for d in range(1, 16):
                scatter(u, d).wait_send()

    for copy in first:
        copy.wait_send()
    for order, u in every:
        for kind in range(4):
            second(order, u, kind).wait_send()
    yield


def along_steps(src, out, sems):
    ring_s, ring_r, peer_s, peer_r = sems
    x, y, z, core = place()
    up, down = (z + 1) % 4, (z + 3) % 4
    positions = (up, 3 - z)
    targets = (up, down)

    def chunk(owner, way, step):
        return out.at[pl.ds(owner, 1), way, step]

    def ring(way, step, block):
        mine = chunk(core, way, step)
        return remote(
            block, mine, ring_s.at[way, step], ring_r.at[way, step], x, y, targets[way], core
        )

    def across(way, step, block):
        mine = chunk(core, way, step)
        return remote(
            block, mine, peer_s.at[way, step], peer_r.at[way, step], x, y, z, 1 - core
        )

    @pl.when(z == 3)
    def _():
        for step in range(CH):
            for way in range(2):
                ring(way, step, src.at[:, way, step]).start()
        for step in range(CH):
            for way in range(2):
                across(way, step, src.at[:, way, step]).start()
        out[pl.ds(core, 1)] = src[...]

    yield
    for tick in range(CH + 2):
        for way in range(2):
            for pos in range(1, 4):
                step = tick - (pos - 1)
                if not 0 <= step < CH:
                    continue

                @pl.when(positions[way] == pos)
                def _():
                    mine = chunk(core, way, step)
                    ring(way, step, mine).wait_recv()
                    if pos < 3:
                        ring(way, step, mine).start()
                    across(way, step, mine).start()

        yield

    for step in range(CH):
        for way in range(2):
            mine, other = chunk(core, way, step), chunk(1 - core, way, step)
            remote(
                mine, other, peer_s.at[way, step], peer_r.at[way, step], x, y, z, 1 - core
            ).wait()

            @pl.when(positions[way] < 3)
            def _():
                ring(way, step, mine).wait_send()

    yield


def reduce_steps(part, wide, src, out, bufs, sems):
    got, acc, tot, got2, fin = bufs
    one_s, one_r, two_s, two_r, g_s, g_r, loc = sems
    x, y, z, core = place()
    units = [unit(part, u, core) for u in range(NP)]
    every = [(order, u) for u in range(NP) for order in range(2)]

    def share(order, u, at, pick):
        p, cols = units[u]
        if order == 0:
            return p, (x + at) % 4, pick, ROWS[0], cols
        return p, pick, (y + at) % 4, ROWS[1], cols

    def one(order, u, kind, way):
        step = 1 if way == 0 else 3
        if kind == 0:
            ref = src.at[share(order, u, 2, PAIR[way])]
        elif kind == 1:
            ref = src.at[share(order, u, step, PAIR[1 - way])]
        else:
            ref = acc.at[order, u, way]
        tx, ty = line(order, x, y, step)
        return remote(
            ref, got.at[order, u, kind, way],
            one_s.at[order, u, kind * 2 + way], one_r.at[order, u, kind * 2 + way],
            tx, ty, z, core,
        )

    for kind in (0, 1):
        for order, u in every:
            for way in range(2):
                one(order, u, kind, way).start()
    yield

    for order, u in every:
        for way in range(2):
            one(order, u, 0, way).wait_recv()
            step = 1 if way == 0 else 3
            acc[order, u, way] = (
                src[share(order, u, step, PAIR[way])] + got[order, u, 0, way]
            )
            one(order, u, 2, way).start()
    yield

    def two(order, u, d):
        tx, ty = line(1 - order, x, y, d)
        index = ty if order == 0 else tx
        return remote(
            tot.at[order, u, index], got2.at[order, u, d - 1],
            two_s.at[order, u, d], two_r.at[order, u, d], tx, ty, z, core,
        )

    for order, u in every:
        for kind in (1, 2):
            for way in range(2):
                one(order, u, kind, way).wait_recv()
        for half in range(2):
            base = src[share(order, u, 0, PAIR[half])]
            tot[order, u, PAIR[half]] = base + (
                got[order, u, 2, half] + got[order, u, 1, 1 - half]
            )
        for d in range(1, 4):
            two(order, u, d).start()
    yield

    for order, u in every:
        for d in range(1, 4):
            two(order, u, d).wait_recv()
        here = y if order == 0 else x
        fin[u, ROWS[order]] = (tot[order, u, here] + got2[order, u, 0]) + (
            got2[order, u, 1] + got2[order, u, 2]
        )

    def slot(u, px, py):
        return out.at[core, u, px, py] if wide else out.at[u, px, py]

    def send(root, u):
        return remote(
            fin.at[u], slot(u, x, y), g_s.at[root, u], g_r.at[u, x * 4 + y], 0, root, z, core
        )

    def keep(u):
        return pltpu.make_async_copy(fin.at[u], slot(u, x, y), loc.at[u])

    def cases():
        for root in range(NP):
            at_root = (x == 0) & (y == root)
            for u in range(NP):
                flag = units[u][0] == root
                if wide:
                    flag = flag | (z == 3)
                yield root, u, flag & at_root, flag & jnp.logical_not(at_root)

    for root, u, local, away in cases():

        @pl.when(away)
        def _():
            send(root, u).start()

        @pl.when(local)
        def _():
            keep(u).start()

    yield

    for root, u, local, away in cases():

        @pl.when(away)
        def _():
            send(root, u).wait_send()

        @pl.when(local)
        def _():
            keep(u).wait()
            for d in range(1, 16):
                sx, sy = (x + d // 4) % 4, (y + d % 4) % 4
                remote(
                    fin.at[u], slot(u, sx, sy), g_s.at[root, u], g_r.at[u, sx * 4 + sy],
                    x, y, z, 1 - core,
                ).wait_recv()

    for order, u in every:
        for kind in range(3):
            for way in range(2):
                one(order, u, kind, way).wait_send()
        for d in range(1, 4):
            two(order, u, d).wait_send()
    yield


DMA = pltpu.SemaphoreType.DMA
SPREAD_SEMS = [
    DMA((3, 16)), DMA((3,)), DMA((2, 3, 4)), DMA((2, 3, 4)), DMA((2, 3, 4)), DMA((2, 3, 4)),
    DMA((3,)),
]
ALONG_SEMS = [DMA((2, CH))] * 4
REDUCE_BUFS = [
    pltpu.VMEM((2, 3, 3, 2, 2, 16, NB), F32),
    pltpu.VMEM((2, 3, 2, 2, 16, NB), F32),
    pltpu.VMEM((2, 3, 4, 16, NB), F32),
    pltpu.VMEM((2, 3, 3, 16, NB), F32),
    pltpu.VMEM((3, 32, NB), F32),
]
REDUCE_SEMS = [
    DMA((2, 3, 6)), DMA((2, 3, 6)), DMA((2, 3, 4)), DMA((2, 3, 4)), DMA((3, 3)), DMA((3, 16)),
    DMA((3,)),
]
VM = pl.BlockSpec(memory_space=pltpu.VMEM)
ANY = pl.BlockSpec(memory_space=pl.ANY)


def drive(*plan):
    for steps, count in plan:
        for _ in range(count):
            next(steps)


def spread_kernel(own, cot, strips, blocks, half, *sems):
    x, y, z, core = place()
    greet(plane_and_peer(x, y, z, core))
    ex_s, ex_r, loc = sems[-3:]
    half_copy = remote(
        cot.at[pl.ds(256 * (1 - core), 256)], half, ex_s.at[3], ex_r.at[3], x, y, z, 1 - core
    )
    half_copy.start()
    steps = spread_steps(0, own, strips, sems[:7])
    drive((steps, 5))
    for u in range(NP):
        p, cols = unit(0, u, core)
        ref = strips.at[p, :, :, :, cols]
        remote(
            ref, blocks.at[core, u], ex_s.at[u], ex_r.at[u], x, y, z, 1 - core
        ).start()
        pltpu.make_async_copy(ref, blocks.at[core, u], loc.at[u]).start()
    drive((steps, 1))
    for u in range(NP):
        p, cols = unit(0, u, core)
        ref = strips.at[p, :, :, :, cols]
        pltpu.make_async_copy(ref, blocks.at[core, u], loc.at[u]).wait()
        remote(
            ref, blocks.at[1 - core, u], ex_s.at[u], ex_r.at[u], x, y, z, 1 - core
        ).wait()
    half_copy.wait()


def comm(collective_id, mib):
    return pltpu.CompilerParams(
        collective_id=collective_id, has_side_effects=True, vmem_limit_bytes=mib << 20
    )


def spread(factor, cot):
    return pl.pallas_call(
        spread_kernel,
        out_shape=(
            jax.ShapeDtypeStruct((3, 4, 4, 32, 1024), F32),
            jax.ShapeDtypeStruct((2, 3, 4, 4, 32, NB), F32),
            jax.ShapeDtypeStruct((256, 1024), F32),
        ),
        in_specs=[ANY, ANY],
        out_specs=(ANY, VM, VM),
        scratch_shapes=SPREAD_SEMS + [DMA((4,)), DMA((4,)), DMA((3,))],
        compiler_params=comm(0, 32),
    )(factor.reshape(4, 4, 32, 1024), cot)


def with_z(x, y, z, core):
    return plane_and_peer(x, y, z, core) + [
        (x, y, (z + 1) % 4, core), (x, y, (z + 3) % 4, core)
    ]


def along_spread_kernel(src, own, _, out, strips, *sems):
    greet(with_z(*place()))
    a = along_steps(src, out, sems[7:])
    s = spread_steps(1, own, strips, sems[:7])
    drive((a, 1), (s, 1), (a, 2), (s, 1), (a, 2), (s, 1), (a, 4), (s, 1), (a, 2), (a, 1), (s, 2))


def along_spread(half, factor, strips):
    out, strips = pl.pallas_call(
        along_spread_kernel,
        out_shape=(
            jax.ShapeDtypeStruct((2, 2, CH, CR, 1536), F32),
            jax.ShapeDtypeStruct((3, 4, 4, 32, 1024), F32),
        ),
        in_specs=[VM, ANY, ANY],
        out_specs=(VM, ANY),
        scratch_shapes=SPREAD_SEMS + ALONG_SEMS,
        input_output_aliases={2: 1},
        compiler_params=comm(1, 16),
    )(half.reshape(1, 2, CH, CR, 1536), factor.reshape(4, 4, 32, 1024), strips)
    return out.reshape(512, 1536), strips.reshape(1536, 1024)


def reduce_kernel(src, out, *rest):
    x, y, z, core = place()
    greet(plane_and_peer(x, y, z, core))
    bufs, sems = rest[:5], rest[5:]
    ex_s, ex_r = sems[-2:]
    steps = reduce_steps(0, True, src, out, bufs, sems[:7])
    drive((steps, 5))

    @pl.when((x == 0) & (y < NP) & (z == 3))
    def _():
        remote(
            out.at[core], out.at[core], ex_s.at[0], ex_r.at[0], x, y, z, 1 - core
        ).start()
        remote(
            out.at[core], out.at[1 - core], ex_s.at[0], ex_r.at[0], x, y, z, 1 - core
        ).wait()


def reduce_rows(part):
    return pl.pallas_call(
        reduce_kernel,
        out_shape=jax.ShapeDtypeStruct((2, 3, 4, 4, 32, NB), F32),
        in_specs=[VM],
        out_specs=VM,
        scratch_shapes=REDUCE_BUFS + REDUCE_SEMS + [DMA((1,)), DMA((1,))],
        compiler_params=comm(2, 32),
    )(part.reshape(3, 4, 4, 32, 1024))


def along_reduce_kernel(src, part, out, rest_out, *rest):
    greet(with_z(*place()))
    bufs, sems = rest[:5], rest[5:]
    a = along_steps(src, out, sems[7:])
    r = reduce_steps(1, False, part, rest_out, bufs, sems[:7])
    drive((a, 1), (r, 1), (a, 2), (r, 1), (a, 3), (r, 1), (a, 1), (r, 1), (a, 4), (a, 1), (r, 1))


def along_reduce(half, part):
    out, rest_out = pl.pallas_call(
        along_reduce_kernel,
        out_shape=(
            jax.ShapeDtypeStruct((2, 2, CH, CR, 1536), F32),
            jax.ShapeDtypeStruct((3, 4, 4, 32, NB), F32),
        ),
        in_specs=[VM, VM],
        out_specs=(VM, VM),
        scratch_shapes=REDUCE_BUFS + REDUCE_SEMS + ALONG_SEMS,
        compiler_params=comm(3, 40),
    )(half.reshape(1, 2, CH, CR, 1536), part.reshape(3, 4, 4, 32, 1024))
    return out.reshape(512, 1536), rest_out.reshape(3, NB, NB)


BS = 128


def invert_kernel(d_ref, o_ref):
    rows = lax.broadcasted_iota(jnp.int32, (BS, BS), 0)
    cols = lax.broadcasted_iota(jnp.int32, (BS, BS), 1)
    diag = rows == cols
    for block in range(NP * (NB // BS)):
        which, at = block // (NB // BS), pl.ds(block % (NB // BS) * BS, BS)
        base = d_ref[which, at, at]
        scale = jnp.sum(jnp.where(diag, base, 0.0), axis=1, keepdims=True)
        o_ref[which, at, at] = jnp.where(diag, 1.0 / scale, 0.0)

    def level(step, carry):
        pick = ((rows >> (step + 1)) == (cols >> (step + 1))) & (
            ((rows >> step) & 1) > ((cols >> step) & 1)
        )
        for block in range(NP * (NB // BS)):
            which, at = block // (NB // BS), pl.ds(block % (NB // BS) * BS, BS)
            have = o_ref[which, at, at]
            below = jnp.where(pick, d_ref[which, at, at], 0.0)
            o_ref[which, at, at] = have - dot(dot(have, below, HI), have, HI)
        return carry

    lax.fori_loop(0, 7, level, 0)
    size = BS
    while size < NB:
        for which in range(NP):
            for base in range(0, NB, 2 * size):
                up, down = pl.ds(base, size), pl.ds(base + size, size)
                corner = dot(
                    dot(o_ref[which, down, down], d_ref[which, down, up], HI),
                    o_ref[which, up, up], HI,
                )
                o_ref[which, down, up] = -corner
                o_ref[which, up, down] = jnp.zeros((size, size), F32)
        size *= 2


def invert(blocks):
    vm = pl.BlockSpec(memory_space=pltpu.VMEM)
    return pl.pallas_call(
        invert_kernel,
        out_shape=jax.ShapeDtypeStruct((NP, NB, NB), F32),
        in_specs=[vm],
        out_specs=vm,
        compiler_params=pltpu.CompilerParams(vmem_limit_bytes=16 << 20),
    )(blocks)


def plan():
    rows = []
    l00, l10, l20, l11, l21, l22, t00, t10, t20, t11, t21, t22, i0, i1, i2 = range(15)
    w, p, q, a2, y2, s21, s21t, a1, y1, s20, s10, s20t, s10t, a0, y0 = range(15, 30)

    def mm(a, b, to, tril=0, half=0):
        rows.append((0, a, b, to, to, tril, 0, 1, half))

    def take(a, b, to):
        rows.append((0, a, b, to, to, 0, 1, -1, 0))

    def turn(a, to, add=0):
        rows.append((1, a, a, a, to, 0, add, 1, 0))

    def adjoint(l, i, t, a, y):
        turn(l, w)
        mm(w, t, p, tril=1, half=1)
        turn(i, w)
        mm(w, p, q)
        mm(q, i, a, half=1)
        turn(a, y, add=1)

    adjoint(l22, i2, t22, a2, y2)
    take(y2, l21, t21)
    take(y2, l20, t20)
    mm(t21, i1, s21)
    turn(s21, s21t)
    take(s21t, l21, t11)
    take(s21t, l20, t10)
    adjoint(l11, i1, t11, a1, y1)
    take(y1, l10, t10)
    take(s21, l10, t20)
    mm(t20, i0, s20)
    mm(t10, i0, s10)
    turn(s20, s20t)
    turn(s10, s10t)
    take(s20t, l20, t00)
    take(s10t, l10, t00)
    adjoint(l00, i0, t00, a0, y0)
    coupling = ((y0, s10t, s20t), (s10, y1, s21t), (s20, s21, y2))
    result = ((a0, a0, a0), (s10, a1, a1), (s20, s21, a2))
    return rows, [x + y for x, y in zip(coupling, result)]


PLAN, PICKS = plan()
BLK = 256


def chain_kernel(plan_ref, pick_ref, l_ref, t_ref, i_ref, q_ref, z_ref, m, high, low):
    row, col = lax.axis_index("row"), lax.axis_index("col")
    for n in range(6):
        m[n] = l_ref[n]
        m[6 + n] = t_ref[n]
    for n in range(3):
        m[12 + n] = i_ref[n]

    def op(n, carry):
        kind, a, b, c = (plan_ref[n, j] for j in range(4))
        to, tril, keep, sign, half = (plan_ref[n, j] for j in range(4, 9))

        @pl.when(kind == 0)
        def _():
            def split(i, carry):
                at = pl.ds(pl.multiple_of(i * 128, 128), 128)
                rows = lax.broadcasted_iota(jnp.int32, (128, NB), 0) + i * 128
                cols = lax.broadcasted_iota(jnp.int32, (128, NB), 1)
                value = jnp.where((cols - rows) * tril > 0, 0.0, m[b, at])
                top = value.astype(jnp.bfloat16)
                high[at] = top
                low[at] = (value - top.astype(F32)).astype(jnp.bfloat16)
                return carry

            lax.fori_loop(0, 4, split, 0)

            def product(i, carry):
                at = pl.ds(pl.multiple_of(i * BLK, BLK), BLK)
                value = m[a, at]
                top = value.astype(jnp.bfloat16)
                rest = (value - top.astype(F32)).astype(jnp.bfloat16)
                right = high[...]
                total = jnp.dot(rest, right, preferred_element_type=F32)
                total += jnp.dot(top, low[...], preferred_element_type=F32)
                total += jnp.dot(top, right, preferred_element_type=F32)
                rows = lax.broadcasted_iota(jnp.int32, (BLK, NB), 0) + i * BLK
                cols = lax.broadcasted_iota(jnp.int32, (BLK, NB), 1)
                total = total * sign.astype(F32)
                halved = jnp.where(rows > cols, total, jnp.where(rows == cols, 0.5 * total, 0.0))
                total = jnp.where(half > 0, halved, total)
                m[to, at] = jnp.where(keep > 0, m[c, at], 0.0) + total
                return carry

            lax.fori_loop(0, NB // BLK, product, 0)

        @pl.when(kind == 1)
        def _():
            def turn(i, carry):
                at = pl.ds(pl.multiple_of(i * 128, 128), 128)
                m[to, :, at] = m[a, at].T + jnp.where(keep > 0, m[a, :, at], 0.0)
                return carry

            lax.fori_loop(0, 4, turn, 0)

        return carry

    lax.fori_loop(0, len(PLAN), op, 0)
    p = jnp.minimum(row, 2)
    half = pl.ds(pl.multiple_of(col % 2 * 256, 256), 256)
    for j in range(3):
        q_ref[:, j * NB : (j + 1) * NB] = m[pick_ref[p, j], half]
        z_ref[j] = m[pick_ref[p, 3 + j]]


def chain(blocks, near, inv):
    smem = pl.BlockSpec(memory_space=pltpu.SMEM)
    return pl.pallas_call(
        chain_kernel,
        out_shape=(
            jax.ShapeDtypeStruct((256, 3 * NB), F32),
            jax.ShapeDtypeStruct((3, NB, NB), F32),
        ),
        in_specs=[smem, smem, VM, VM, VM],
        out_specs=(VM, VM),
        scratch_shapes=[
            pltpu.VMEM((30, NB, NB), F32),
            pltpu.VMEM((NB, NB), jnp.bfloat16),
            pltpu.VMEM((NB, NB), jnp.bfloat16),
        ],
        compiler_params=pltpu.CompilerParams(vmem_limit_bytes=56 << 20),
    )(jnp.array(PLAN, jnp.int32), jnp.array(PICKS, jnp.int32), blocks, near, inv)


def shards(factor, cot):
    row = lax.axis_index("row")
    col = lax.axis_index("col")
    core = col % 2
    strips, blocks, other_half = spread(factor, cot)
    blocks = blocks.reshape(2, 3, NB, NB)
    l = {
        0: blocks[0, 0], 10: blocks[0, 1], 20: blocks[0, 2],
        11: blocks[1, 0], 21: blocks[1, 1], 22: blocks[1, 2],
    }
    inv = invert(jnp.stack([l[0], l[11], l[22]]))
    my_half = lax.dynamic_slice(cot, (core * 256, 0), (256, 1024))
    g6 = jnp.where(core == 0, my_half, other_half)
    g7 = jnp.where(core == 0, other_half, my_half)
    s2 = dot(g7[:, NB:], inv[2])
    s1 = dot(g7[:, :NB] - dot(s2, l[21]), inv[1])
    s0 = dot(g6[:, NB:] - dot(s2, l[20]) - dot(s1, l[10]), inv[0])
    solved, strips = along_spread(jnp.concatenate([s0, s1, s2], axis=1), factor, strips)
    lower_rows = row >= NP
    part = jnp.where(lower_rows, -dot_t(solved, factor), 0.0).reshape(3, NB, 1024)
    which = lax.broadcasted_iota(jnp.int32, (3, 1, 1), 0)
    part = jnp.where(which == row, cot[None], part)
    near = reduce_rows(part).reshape(2, 3, NB, NB)
    mixed_half, z = chain(blocks.reshape(6, NB, NB), near.reshape(6, NB, NB), inv)
    mixed, far = along_reduce(mixed_half, part)
    factor_rows = jnp.where(lower_rows, solved, mixed)
    even = core == 0

    def by_row(zero, one, two):
        return jnp.where(row == 0, zero, jnp.where(row == 1, one, two))

    total_left = by_row(
        far[0], jnp.where(even, far[1], near[1, 0]), jnp.where(even, far[2], near[1, 1])
    )
    total_right = by_row(
        jnp.where(even, near[0, 0], far[1]),
        jnp.where(even, near[0, 1], far[2]),
        jnp.where(even, near[0, 2], near[1, 2]),
    )
    start = jnp.where(
        lower_rows, cot, jnp.concatenate([total_left, total_right], axis=1)
    )
    out = start - dot(factor_rows, strips)
    last6 = jnp.where(lower_rows, solved[:, :NB], z[0])
    left7 = jnp.where(
        lower_rows, solved[:, NB:1024], jnp.where(row == 0, cot[:, :NB], z[1])
    )
    right7 = jnp.where(
        lower_rows, solved[:, 1024:], jnp.where(row == 2, z[2], cot[:, NB:])
    )
    left = jnp.where(col == 7, left7, out[:, :NB])
    right = jnp.where(col == 7, right7, jnp.where(col == 6, last6, out[:, NB:]))
    return jnp.concatenate([left, right], axis=1)


def solution(mesh):
    placed = (P("row", "col"), P("row", "col"))
    return jax.shard_map(
        shards, mesh=mesh, in_specs=placed, out_specs=P("row", "col"), check_vma=False
    )
```

profile of v0, /device:TPU:1, one launch (start us, length us, event | category | flops | bytes accessed | tf_op | source)
XLA Modules:
  0.0 341.1 jit_solution(9613665642365186332)
XLA Ops:
  0.0 1.6 copy-done.1
  1.6 1.6 copy-done.10
  3.2 49.9 %shard_map.46 = (f32[3,4,4,32,1024]{4,3,2,1,0:T(8,128)S(1)}, f32[2,3,4,4,32,512]{5,4,3,2,1,0:T(8,128)S(1)}, f32[256,1024]{1,0:T(8,128)S(1)}) custom-call(f32[4,4,32,1024]{3,2,1,0:T(8,128)S(1)} %bitcast.108, f32[512,1024]{1,0:T(8,128)S(1)} %copy-done.1), custom_call_target="tpu_custom_call" | custom-call | tf_op jit(solution)/shard_map/pallas_call | solution.py:460
  53.1 2.6 copy-done.8
  56.2 2.1 copy-done.7
  59.0 14.4 %shard_map.47.i_ref = f32[3,512,512]{2,1,0:T(8,128)S(1)} custom-call(f32[3,512,512]{2,1,0:T(8,128)S(1)} %pad_maximum_fusion.d_ref), custom_call_target="tpu_custom_call" | custom-call | tf_op jit(solution)/shard_map/pallas_call | solution.py:596
  73.4 1.8 fusion.13
  75.2 2.4 convolution_subtract_fusion.2
  77.7 2.0 convolution_subtract_fusion.1
  80.3 2.0 convolution_subtract_fusion
  84.0 48.6 %shard_map.48 = (f32[2,2,8,16,1536]{4,3,2,1,0:T(8,128)S(1)}, f32[3,4,4,32,1024]{4,3,2,1,0:T(8,128)S(1)}) custom-call(f32[1,2,8,16,1536]{4,3,2,1,0:T(8,128)S(1)} %bitcast.110, f32[4,4,32,1024]{3,2,1,0:T(8,128)S(1)} %bitcast.109, f32[3,4,4,32,1024]{4,3,2,1,0:T(8,128)S(1)} %bitcast.106), custom_call_target="tpu_custom_call", output_to_operand_aliasing={{1}: (2, {})} | custom-call | tf_op jit(solution)/shard_map/pallas_call | solution.py:488
  132.6 2.6 copy-done.9
  135.2 8.0 %negate_select_fusion = f32[1536,1024]{1,0:T(8,128)S(1)} fusion(f32[512,1536]{1,0:T(8,128)S(1)} %bitcast.98, f32[512,1024]{1,0:T(8,128)} %param.4, pred[]{:T(512)S(6)} %ge.3), kind=kOutput, calls=%fused_computation | convolution fusion | flops 4834983936 | bytes 11534337 | tf_op jit(solution)/shard_map/dot_general | solution.py:21
  144.2 38.5 %shard_map.49 = f32[2,3,4,4,32,512]{5,4,3,2,1,0:T(8,128)S(1)} custom-call(f32[3,4,4,32,1024]{4,3,2,1,0:T(8,128)S(1)} %broadcast_select_fusion.src.part), custom_call_target="tpu_custom_call" | custom-call | tf_op jit(solution)/shard_map/pallas_call | solution.py:522
  182.7 2.6 copy-done
  185.3 49.7 %shard_map.50 = (f32[256,1536]{1,0:T(8,128)}, f32[3,512,512]{2,1,0:T(8,128)}) custom-call(s32[32,9]{1,0:T(8,128)} %constant.40.clone.plan_ref, s32[3,6]{1,0:T(4,128)} %constant.41.clone.pick_ref, f32[6,512,512]{2,1,0:T(8,128)} %bitcast.104, f32[6,512,512]{2,1,0:T(8,128)} %bitcast.95, f32[3,512,512]{2,1,0:T(8,128)} %copy-done.6), custom_call_target="tpu_custom_call" | custom-call | tf_op jit(solution)/shard_map/pallas_call | solution.py:719
  235.0 1.4 copy-done.13
  236.5 80.7 %shard_map.51 = (f32[2,2,8,16,1536]{4,3,2,1,0:T(8,128)S(1)}, f32[3,4,4,32,512]{4,3,2,1,0:T(8,128)S(1)}) custom-call(f32[1,2,8,16,1536]{4,3,2,1,0:T(8,128)S(1)} %bitcast.111, f32[3,4,4,32,1024]{4,3,2,1,0:T(8,128)S(1)} %broadcast_select_fusion.src.part), custom_call_target="tpu_custom_call" | custom-call | tf_op jit(solution)/shard_map/pallas_call | solution.py:541
  317.2 2.5 broadcast_select_fusion.1
  319.7 1.8 fusion.15
  321.5 4.7 %fusion.9 = (f32[512,512]{1,0:T(8,128)S(1)}, f32[512,512]{1,0:T(8,128)S(1)}) fusion(f32[2,3,512,512]{3,2,1,0:T(8,128)} %bitcast.96, f32[1,4,4,32,512]{4,3,2,1,0:T(8,128)} %get-tuple-element.31, f32[1,4,4,32,512]{4,3,2,1,0:T(8,128)} %get-tuple-element.32, f32[1,4,4,32,512]{4,3,2,1,0:T(8,128)S(1)} %get-tuple-element.30, pred[]{:T(512)S(6)} %eq.38, ...), kind=kLoop, calls=%fused_computation.27 | loop fusion | flops 2359296 | bytes 11536384 | tf_op jit(solution)/shard_map/jit(_where)/select_n | solution.py:765
  326.5 8.5 %fusion = f32[512,1024]{1,0:T(8,128)} fusion(f32[512,1024]{1,0:T(8,128)S(1)} %copy-done.3, f32[512,512]{1,0:T(8,128)S(1)} %get-tuple-element.26, f32[512,512]{1,0:T(8,128)S(1)} %get-tuple-element.25, f32[512,1536]{1,0:T(8,128)S(1)} %bitcast.113, f32[1536,1024]{1,0:T(8,128)} %bitcast.107, pred[]{:T(512)S(6)} %ge.3), kind=kOutput, calls=%fused_computation.4 | convolution fusion | flops 4833411072 | bytes 15728641 | tf_op jit(solution)/shard_map/dot_general | solution.py:17
  334.9 4.7 %slice_select_fusion.3 = (f32[512,512]{1,0:T(8,128)S(1)}, f32[512,512]{1,0:T(8,128)S(1)}) fusion(f32[512,1024]{1,0:T(8,128)} %fusion, f32[512,1536]{1,0:T(8,128)} %bitcast.99, f32[3,512,512]{2,1,0:T(8,128)} %get-tuple-element.18, f32[512,1024]{1,0:T(8,128)S(1)} %copy-done.3, pred[]{:T(512)S(6)} %eq.39, pred[]{:T(512)S(6)} %ge.3, pred[]{:T(512)S(6)} %eq.37, ...), kind=kLoop, calls=%fused_computation.15 | loop fusion | flops 2097152 | bytes 12582917 | tf_op jit(solution)/shard_map/jit(_where)/select_n | solution.py:786
  339.7 1.5 pad_maximum_fusion.1
  (42 shorter events, 4.6 us)
Async XLA Ops:
  0.0 1.6 copy-start.1
  1.6 1.6 copy-start.10
  53.1 2.6 copy-start.8
  55.7 2.6 copy-start.7
  55.7 3.0 copy-start.12
  55.9 17.5 %copy-start.16 = (f32[256,1024]{1,0:T(8,128)}, f32[256,1024]{1,0:T(8,128)S(1)}, u32[]{:S(2)}) copy-start(f32[256,1024]{1,0:T(8,128)S(1)} %dynamic-slice_select_fusion) | copy-start | bytes 3145732
  73.4 8.9 %copy-start.6 = (f32[3,512,512]{2,1,0:T(8,128)}, f32[3,512,512]{2,1,0:T(8,128)S(1)}, u32[]{:S(2)}) copy-start(f32[3,512,512]{2,1,0:T(8,128)S(1)} %shard_map.47.i_ref) | copy-start | bytes 9437188
  75.2 2.4 copy-start.15
  75.2 2.4 copy-start.17
  77.7 5.4 %slice-start = ((s8[6291456]{0:T(1024)(128)(4,1)}), s8[4194304]{0:T(1024)(128)(4,1)S(1)}, s32[]{:S(2)}) async-start(s8[6291456]{0:T(1024)(128)(4,1)} %bitcast.105), calls=%async_computation | async-start | bytes 8388608
  80.3 2.8 slice-start.1
  82.4 1.6 copy-start.11
  132.6 2.6 copy-start.9
  135.2 8.0 %copy-start.4 = (f32[2,2,8,16,1536]{4,3,2,1,0:T(8,128)}, f32[2,2,8,16,1536]{4,3,2,1,0:T(8,128)S(1)}, u32[]{:S(2)}) copy-start(f32[2,2,8,16,1536]{4,3,2,1,0:T(8,128)S(1)} %get-tuple-element.17) | copy-start | bytes 9437188
  135.2 8.0 %copy-start.2 = (f32[512,1024]{1,0:T(8,128)S(1)}, f32[512,1024]{1,0:T(8,128)}, u32[]{:S(2)}) copy-start(f32[512,1024]{1,0:T(8,128)} %cot.1) | copy-start | bytes 6291460
  182.7 2.6 copy-start
  235.0 1.4 copy-start.13
  236.5 80.7 %copy-start.5 = (f32[2,2,8,16,1536]{4,3,2,1,0:T(8,128)S(1)}, f32[2,2,8,16,1536]{4,3,2,1,0:T(8,128)}, u32[]{:S(2)}) copy-start(f32[2,2,8,16,1536]{4,3,2,1,0:T(8,128)} %copy-done.4) | copy-start | bytes 9437188
  321.5 4.7 %copy-start.3 = (f32[512,1024]{1,0:T(8,128)S(1)}, f32[512,1024]{1,0:T(8,128)}, u32[]{:S(2)}) copy-start(f32[512,1024]{1,0:T(8,128)} %cot.1) | copy-start | bytes 6291460
  321.5 5.0 %copy-start.14 = (f32[2,2,8,16,1536]{4,3,2,1,0:T(8,128)S(1)}, f32[2,2,8,16,1536]{4,3,2,1,0:T(8,128)}, u32[]{:S(2)}) copy-start(f32[2,2,8,16,1536]{4,3,2,1,0:T(8,128)} %broadcast_select_fusion.1) | copy-start | bytes 9437188
where the time goes:
time: 341 us
  Pallas kernels  282 us (83%)
  matrix products  25.9 us (8%)
  local copies, waits for them, and re-layouts  18.1 us (5%)
  other arithmetic  14.9 us (4%)
    pallas_call x1, Pallas kernels, along_reduce(): pl.pallas_call(along_reduce_kernel, out_shape=(jax.ShapeDtypeStruct((2, 2...  80.7 us
    pallas_call x1, Pallas kernels, spread(): pl.pallas_call(spread_kernel, out_shape=(jax.ShapeDtypeStruct((3, 4, 4, 3...  49.9 us
    pallas_call x1, Pallas kernels, chain(): pl.pallas_call(chain_kernel, out_shape=(jax.ShapeDtypeStruct((256, 3 * NB...  49.7 us
    pallas_call x1, Pallas kernels, along_spread(): pl.pallas_call(along_spread_kernel, out_shape=(jax.ShapeDtypeStruct((2, 2...  48.6 us
    pallas_call x1, Pallas kernels, reduce_rows(): pl.pallas_call(reduce_kernel, out_shape=jax.ShapeDtypeStruct((2, 3, 4, 4,...  38.5 us
    dot_general x7, matrix products, dot(): return jnp.dot(a, b, precision=precision, preferred_element_type=F32)  17.9 us
    unnamed x40, local copies, waits for them, and re-layouts  16 us
    pallas_call x1, Pallas kernels, invert(): pl.pallas_call(invert_kernel, out_shape=jax.ShapeDtypeStruct((NP, NB, NB)...  14.4 us

commit v1 on v0

--- a/solution.py
+++ b/solution.py
@@ -201,12 +201,16 @@
     yield
 
 
-def along_steps(src, out, sems):
+AHEAD = 3
+
+
+def along_steps(src, out, sems, used):
     ring_s, ring_r, peer_s, peer_r = sems
     x, y, z, core = place()
     up, down = (z + 1) % 4, (z + 3) % 4
     positions = (up, 3 - z)
     targets = (up, down)
+    source = used & (z == 3)
 
     def chunk(owner, way, step):
         return out.at[pl.ds(owner, 1), way, step]
@@ -223,25 +227,35 @@
             block, mine, peer_s.at[way, step], peer_r.at[way, step], x, y, z, 1 - core
         )
 
-    @pl.when(z == 3)
+    def issue(step):
+        for way in range(2):
+            ring(way, step, src.at[:, way, step]).start()
+        for way in range(2):
+            across(way, step, src.at[:, way, step]).start()
+
+    @pl.when(source)
     def _():
-        for step in range(CH):
-            for way in range(2):
-                ring(way, step, src.at[:, way, step]).start()
-        for step in range(CH):
-            for way in range(2):
-                across(way, step, src.at[:, way, step]).start()
+        for step in range(AHEAD):
+            issue(step)
         out[pl.ds(core, 1)] = src[...]
 
     yield
     for tick in range(CH + 2):
+        if tick + AHEAD < CH:
+
+            @pl.when(source)
+            def _():
+                for way in range(2):
+                    ring(way, tick, src.at[:, way, tick]).wait_send()
+                issue(tick + AHEAD)
+
         for way in range(2):
             for pos in range(1, 4):
                 step = tick - (pos - 1)
                 if not 0 <= step < CH:
                     continue
 
-                @pl.when(positions[way] == pos)
+                @pl.when(used & (positions[way] == pos))
                 def _():
                     mine = chunk(core, way, step)
                     ring(way, step, mine).wait_recv()
@@ -251,16 +265,22 @@
 
         yield
 
-    for step in range(CH):
-        for way in range(2):
-            mine, other = chunk(core, way, step), chunk(1 - core, way, step)
-            remote(
-                mine, other, peer_s.at[way, step], peer_r.at[way, step], x, y, z, 1 - core
-            ).wait()
-
-            @pl.when(positions[way] < 3)
-            def _():
-                ring(way, step, mine).wait_send()
+    @pl.when(used)
+    def _():
+        for step in range(CH):
+            for way in range(2):
+                mine, other = chunk(core, way, step), chunk(1 - core, way, step)
+                remote(
+                    mine, other, peer_s.at[way, step], peer_r.at[way, step],
+                    x, y, z, 1 - core,
+                ).wait()
+                left = positions[way] < 3
+                if step + AHEAD < CH:
+                    left = left & (z != 3)
+
+                @pl.when(left)
+                def _():
+                    ring(way, step, mine).wait_send()
 
     yield
 
@@ -479,9 +499,9 @@
 
 def along_spread_kernel(src, own, _, out, strips, *sems):
     greet(with_z(*place()))
-    a = along_steps(src, out, sems[7:])
+    a = along_steps(src, out, sems[7:], lax.axis_index("row") >= NP)
     s = spread_steps(1, own, strips, sems[:7])
-    drive((a, 1), (s, 1), (a, 2), (s, 1), (a, 2), (s, 1), (a, 4), (s, 1), (a, 2), (a, 1), (s, 2))
+    drive((s, 1), (a, 1), (a, 2), (s, 1), (a, 2), (s, 1), (a, 4), (s, 1), (a, 2), (a, 1), (s, 2))
 
 
 def along_spread(half, factor, strips):
@@ -532,9 +552,9 @@
 def along_reduce_kernel(src, part, out, rest_out, *rest):
     greet(with_z(*place()))
     bufs, sems = rest[:5], rest[5:]
-    a = along_steps(src, out, sems[7:])
+    a = along_steps(src, out, sems[7:], lax.axis_index("row") < NP)
     r = reduce_steps(1, False, part, rest_out, bufs, sems[:7])
-    drive((a, 1), (r, 1), (a, 2), (r, 1), (a, 3), (r, 1), (a, 1), (r, 1), (a, 4), (a, 1), (r, 1))
+    drive((a, 1), (r, 1), (a, 3), (r, 1), (a, 3), (r, 1), (a, 1), (r, 1), (a, 3), (a, 1), (r, 1))
 
 
 def along_reduce(half, part):
@@ -731,6 +751,107 @@
         ],
         compiler_params=pltpu.CompilerParams(vmem_limit_bytes=56 << 20),
     )(jnp.array(PLAN, jnp.int32), jnp.array(PICKS, jnp.int32), blocks, near, inv)
+
+
+def finish_kernel(cot, solved, mixed, strips, far, near, z, out, high, low, f_high, f_low):
+    row, col = lax.axis_index("row"), lax.axis_index("col")
+    core = col % 2
+    r = jnp.minimum(row, 2)
+    lower_rows = row >= NP
+
+    @pl.when(col < 7)
+    def _():
+        def split(i, carry):
+            at = pl.ds(pl.multiple_of(i * 128, 128), 128)
+            value = jnp.where(lower_rows, solved[at], mixed[at])
+            top = value.astype(jnp.bfloat16)
+            f_high[at] = top
+            f_low[at] = (value - top.astype(F32)).astype(jnp.bfloat16)
+            return carry
+
+        lax.fori_loop(0, 4, split, 0)
+
+    for h in range(2):
+        cols = pl.ds(h * NB, NB)
+        if h == 0:
+            use_far = (core == 0) | (row == 0)
+            at_far = r * (1 - core)
+            at_near = jnp.maximum(r - core, 0)
+            plain = col < 7
+        else:
+            use_far = (core == 1) & (row < 2)
+            at_far = jnp.minimum(r + 1, 2)
+            at_near = r * (1 - core) + 2 * core
+            plain = col < 6
+
+        @pl.when(plain)
+        def _():
+            def begin(i, carry):
+                at = pl.ds(pl.multiple_of(i * 128, 128), 128)
+                total = jnp.where(use_far, far[at_far, at], near[core, at_near, at])
+                out[at, cols] = jnp.where(lower_rows, cot[at, cols], total)
+                return carry
+
+            lax.fori_loop(0, 4, begin, 0)
+
+            def deep(k, carry):
+                def split(i, carry):
+                    at = pl.ds(pl.multiple_of(i * 128, 128), 128)
+                    from_at = pl.ds(pl.multiple_of(k * NB + i * 128, 128), 128)
+                    value = strips[from_at, cols]
+                    top = value.astype(jnp.bfloat16)
+                    high[at] = top
+                    low[at] = (value - top.astype(F32)).astype(jnp.bfloat16)
+                    return carry
+
+                lax.fori_loop(0, 4, split, 0)
+                inner = pl.ds(pl.multiple_of(k * NB, NB), NB)
+
+                def product(i, carry):
+                    at = pl.ds(pl.multiple_of(i * BLK, BLK), BLK)
+                    top, rest, right = f_high[at, inner], f_low[at, inner], high[...]
+                    total = jnp.dot(rest, right, preferred_element_type=F32)
+                    total += jnp.dot(top, low[...], preferred_element_type=F32)
+                    total += jnp.dot(top, right, preferred_element_type=F32)
+                    out[at, cols] = out[at, cols] - total
+                    return carry
+
+                lax.fori_loop(0, NB // BLK, product, 0)
+                return carry
+
+            lax.fori_loop(0, NP, deep, 0)
+
+        @pl.when(jnp.logical_not(plain))
+        def _():
+            def move(i, carry):
+                at = pl.ds(pl.multiple_of(i * 128, 128), 128)
+                if h == 0:
+                    upper = jnp.where(row == 0, cot[at, cols], z[1, at])
+                    out[at, cols] = jnp.where(lower_rows, solved[at, NB : 2 * NB], upper)
+                else:
+                    upper = jnp.where(row == 2, z[2, at], cot[at, cols])
+                    last = jnp.where(lower_rows, solved[at, 2 * NB :], upper)
+                    first = jnp.where(lower_rows, solved[at, :NB], z[0, at])
+                    out[at, cols] = jnp.where(col == 7, last, first)
+                return carry
+
+            lax.fori_loop(0, 4, move, 0)
+
+
+def finish(cot, solved, mixed, strips, far, near, z):
+    return pl.pallas_call(
+        finish_kernel,
+        out_shape=jax.ShapeDtypeStruct((NB, 2 * NB), F32),
+        in_specs=[VM] * 7,
+        out_specs=VM,
+        scratch_shapes=[
+            pltpu.VMEM((NB, NB), jnp.bfloat16),
+            pltpu.VMEM((NB, NB), jnp.bfloat16),
+            pltpu.VMEM((NB, 3 * NB), jnp.bfloat16),
+            pltpu.VMEM((NB, 3 * NB), jnp.bfloat16),
+        ],
+        compiler_params=pltpu.CompilerParams(vmem_limit_bytes=40 << 20),
+    )(cot, solved, mixed, strips, far, near, z)
 
 
 def shards(factor, cot):
@@ -758,34 +879,7 @@
     near = reduce_rows(part).reshape(2, 3, NB, NB)
     mixed_half, z = chain(blocks.reshape(6, NB, NB), near.reshape(6, NB, NB), inv)
     mixed, far = along_reduce(mixed_half, part)
-    factor_rows = jnp.where(lower_rows, solved, mixed)
-    even = core == 0
-
-    def by_row(zero, one, two):
-        return jnp.where(row == 0, zero, jnp.where(row == 1, one, two))
-
-    total_left = by_row(
-        far[0], jnp.where(even, far[1], near[1, 0]), jnp.where(even, far[2], near[1, 1])
-    )
-    total_right = by_row(
-        jnp.where(even, near[0, 0], far[1]),
-        jnp.where(even, near[0, 1], far[2]),
-        jnp.where(even, near[0, 2], near[1, 2]),
-    )
-    start = jnp.where(
-        lower_rows, cot, jnp.concatenate([total_left, total_right], axis=1)
-    )
-    out = start - dot(factor_rows, strips)
-    last6 = jnp.where(lower_rows, solved[:, :NB], z[0])
-    left7 = jnp.where(
-        lower_rows, solved[:, NB:1024], jnp.where(row == 0, cot[:, :NB], z[1])
-    )
-    right7 = jnp.where(
-        lower_rows, solved[:, 1024:], jnp.where(row == 2, z[2], cot[:, NB:])
-    )
-    left = jnp.where(col == 7, left7, out[:, :NB])
-    right = jnp.where(col == 7, right7, jnp.where(col == 6, last6, out[:, NB:]))
-    return jnp.concatenate([left, right], axis=1)
+    return finish(cot, solved, mixed, strips, far, near, z)
 
 
 def solution(mesh):

time: 341 us -> 317 us (0.930)
  matrix products: 25.9 us -> 8.89 us
  other arithmetic: 14.9 us -> 1.64 us
  Pallas kernels: 282 us -> 292 us
  local copies, waits for them, and re-layouts: 18.1 us -> 13.7 us
    pallas_call x0 -> x1, Pallas kernels: none -> 15.7 us  [finish(): pl.pallas_call(finish_kernel, out_shape=jax.ShapeDtypeStruct((NB, 2 * NB)...]
    dot_general x7 -> x6, matrix products: 17.9 us -> 3.69 us  [dot(): return jnp.dot(a, b, precision=precision, preferred_element_type=F32)]
    select_n x3 -> x0, other arithmetic: 11.9 us -> none  [the longest x1 4.72 us: shards(): left = jnp.where(col == 7, left7, out[:, :NB])]
    pallas_call x1, Pallas kernels: 80.7 us -> 74.8 us  [along_reduce(): pl.pallas_call(along_reduce_kernel, out_shape=(jax.ShapeDtypeStruct((2, 2...]
    unnamed x40 -> x26, local copies, waits for them, and re-layouts: 16 us -> 13.4 us
where the time goes in v1:
time: 317 us; the launch traced here: 316 us
  Pallas kernels  292 us (92%)
  local copies, waits for them, and re-layouts  13.7 us (4%)
  matrix products  8.89 us (3%)
    pallas_call x1, Pallas kernels, along_reduce(): pl.pallas_call(along_reduce_kernel, out_shape=(jax.ShapeDtypeStruct((2, 2...  74.8 us
    pallas_call x1, Pallas kernels, spread(): pl.pallas_call(spread_kernel, out_shape=(jax.ShapeDtypeStruct((3, 4, 4, 3...  49.9 us
    pallas_call x1, Pallas kernels, chain(): pl.pallas_call(chain_kernel, out_shape=(jax.ShapeDtypeStruct((256, 3 * NB...  49.7 us
    pallas_call x1, Pallas kernels, along_spread(): pl.pallas_call(along_spread_kernel, out_shape=(jax.ShapeDtypeStruct((2, 2...  48.1 us
    pallas_call x1, Pallas kernels, reduce_rows(): pl.pallas_call(reduce_kernel, out_shape=jax.ShapeDtypeStruct((2, 3, 4, 4,...  39.4 us
    pallas_call x1, Pallas kernels, finish(): pl.pallas_call(finish_kernel, out_shape=jax.ShapeDtypeStruct((NB, 2 * NB)...  15.7 us
    pallas_call x1, Pallas kernels, invert(): pl.pallas_call(invert_kernel, out_shape=jax.ShapeDtypeStruct((NP, NB, NB)...  14.3 us
    unnamed x26, local copies, waits for them, and re-layouts  13.4 us

profile of v1, /device:TPU:1, one launch (start us, length us, event | category | flops | bytes accessed | tf_op | source)
XLA Modules:
  0.0 316.4 jit_solution(17509570762594846540)
XLA Ops:
  0.0 1.6 copy-done.1
  1.6 1.6 copy-done.9
  3.2 49.9 %shard_map.46 = (f32[3,4,4,32,1024]{4,3,2,1,0:T(8,128)S(1)}, f32[2,3,4,4,32,512]{5,4,3,2,1,0:T(8,128)S(1)}, f32[256,1024]{1,0:T(8,128)S(1)}) custom-call(f32[4,4,32,1024]{3,2,1,0:T(8,128)S(1)} %bitcast.55, f32[512,1024]{1,0:T(8,128)S(1)} %copy-done.1), custom_call_target="tpu_custom_call" | custom-call | tf_op jit(solution)/shard_map/pallas_call | solution.py:480
  53.3 0.3 slice_bitcast_fusion.14
  53.6 0.3 pad_maximum_fusion.d_ref
  54.0 14.3 %shard_map.47.i_ref = f32[3,512,512]{2,1,0:T(8,128)S(1)} custom-call(f32[3,512,512]{2,1,0:T(8,128)S(1)} %pad_maximum_fusion.d_ref), custom_call_target="tpu_custom_call" | custom-call | tf_op jit(solution)/shard_map/pallas_call | solution.py:616
  68.3 0.6 fusion.2
  68.9 0.6 convolution_subtract_fusion.2
  69.5 0.6 convolution_subtract_fusion.1
  70.1 0.6 fusion.1
  70.8 0.6 convolution_subtract_fusion
  71.4 0.6 fusion
  72.1 48.1 %shard_map.48 = (f32[2,2,8,16,1536]{4,3,2,1,0:T(8,128)S(1)}, f32[3,4,4,32,1024]{4,3,2,1,0:T(8,128)S(1)}) custom-call(f32[1,2,8,16,1536]{4,3,2,1,0:T(8,128)S(1)} %bitcast.57, f32[4,4,32,1024]{3,2,1,0:T(8,128)S(1)} %bitcast.56, f32[3,4,4,32,1024]{4,3,2,1,0:T(8,128)S(1)} %get-tuple-element.16._), custom_call_target="tpu_custom_call", output_to_operand_aliasing={{1}: (2, {})} | custom-call | tf_op jit(solution)/shard_map/pallas_call | solution.py:508
  120.2 2.7 copy-done.6
  122.9 5.2 %negate_select_fusion = f32[1536,1024]{1,0:T(8,128)S(1)} fusion(f32[512,1536]{1,0:T(8,128)S(1)} %bitcast.53, f32[512,1024]{1,0:T(8,128)S(1)} %copy-done.9, pred[]{:T(512)S(6)} %ge.3), kind=kOutput, calls=%fused_computation | convolution fusion | flops 4834983936 | bytes 11534337 | tf_op jit(solution)/shard_map/dot_general | solution.py:21
  128.1 1.0 broadcast_select_fusion.src.part
  129.1 39.4 %shard_map.49 = f32[2,3,4,4,32,512]{5,4,3,2,1,0:T(8,128)S(1)} custom-call(f32[3,4,4,32,1024]{4,3,2,1,0:T(8,128)S(1)} %broadcast_select_fusion.src.part), custom_call_target="tpu_custom_call" | custom-call | tf_op jit(solution)/shard_map/pallas_call | solution.py:542
  168.6 2.6 copy-done
  171.2 49.7 %shard_map.50 = (f32[256,1536]{1,0:T(8,128)}, f32[3,512,512]{2,1,0:T(8,128)}) custom-call(s32[32,9]{1,0:T(8,128)} %constant.35.clone.plan_ref, s32[3,6]{1,0:T(4,128)} %constant.36.clone.pick_ref, f32[6,512,512]{2,1,0:T(8,128)} %bitcast.51, f32[6,512,512]{2,1,0:T(8,128)} %bitcast.44, f32[3,512,512]{2,1,0:T(8,128)} %copy-done.4), custom_call_target="tpu_custom_call" | custom-call | tf_op jit(solution)/shard_map/pallas_call | solution.py:739
  220.9 1.4 copy-done.12
  222.3 74.8 %shard_map.51 = (f32[2,2,8,16,1536]{4,3,2,1,0:T(8,128)S(1)}, f32[3,4,4,32,512]{4,3,2,1,0:T(8,128)S(1)}) custom-call(f32[1,2,8,16,1536]{4,3,2,1,0:T(8,128)S(1)} %bitcast.60, f32[3,4,4,32,1024]{4,3,2,1,0:T(8,128)S(1)} %broadcast_select_fusion.src.part), custom_call_target="tpu_custom_call" | custom-call | tf_op jit(solution)/shard_map/pallas_call | solution.py:561
  297.1 1.6 copy-done.10
  298.8 1.9 copy-done.11
  300.7 15.7 %shard_map.52 = f32[512,1024]{1,0:T(8,128)} custom-call(f32[512,1024]{1,0:T(8,128)S(1)} %copy-done.3, f32[512,1536]{1,0:T(8,128)S(1)} %bitcast.54, f32[512,1536]{1,0:T(8,128)S(1)} %bitcast.58, f32[1536,1024]{1,0:T(8,128)} %bitcast.52, f32[3,512,512]{2,1,0:T(8,128)S(1)} %bitcast.59, f32[2,3,512,512]{3,2,1,0:T(8,128)} %bitcast.45, ...), custom_call_target="tpu_custom_call" | custom-call | tf_op jit(solution)/shard_map/pallas_call | solution.py:842
  (22 shorter events, 0.3 us)
Async XLA Ops:
  0.0 1.6 copy-start.1
  1.6 1.6 copy-start.9
  53.1 17.7 %copy-start.5 = (f32[2,3,4,4,32,512]{5,4,3,2,1,0:T(8,128)}, f32[2,3,4,4,32,512]{5,4,3,2,1,0:T(8,128)S(1)}, u32[]{:S(2)}) copy-start(f32[2,3,4,4,32,512]{5,4,3,2,1,0:T(8,128)S(1)} %get-tuple-element.15) | copy-start | bytes 18874372
  68.3 3.1 copy-start.4
  120.2 2.7 copy-start.6
  122.9 5.2 %copy-start.7 = (f32[2,2,8,16,1536]{4,3,2,1,0:T(8,128)}, f32[2,2,8,16,1536]{4,3,2,1,0:T(8,128)S(1)}, u32[]{:S(2)}) copy-start(f32[2,2,8,16,1536]{4,3,2,1,0:T(8,128)S(1)} %get-tuple-element.17) | copy-start | bytes 9437188
  122.9 5.2 %copy-start.2 = (f32[512,1024]{1,0:T(8,128)S(1)}, f32[512,1024]{1,0:T(8,128)}, u32[]{:S(2)}) copy-start(f32[512,1024]{1,0:T(8,128)} %cot.3) | copy-start | bytes 6291460
  168.6 2.6 copy-start
  220.9 1.4 copy-start.12
  222.3 76.5 %copy-start.3 = (f32[512,1024]{1,0:T(8,128)S(1)}, f32[512,1024]{1,0:T(8,128)}, u32[]{:S(2)}) copy-start(f32[512,1024]{1,0:T(8,128)} %cot.3) | copy-start | bytes 6291460
  222.3 76.5 %copy-start.8 = (f32[2,2,8,16,1536]{4,3,2,1,0:T(8,128)S(1)}, f32[2,2,8,16,1536]{4,3,2,1,0:T(8,128)}, u32[]{:S(2)}) copy-start(f32[2,2,8,16,1536]{4,3,2,1,0:T(8,128)} %copy-done.7) | copy-start | bytes 9437188
  297.1 1.7 copy-start.10
  298.8 1.9 copy-start.11

commit v2 on v1

--- a/solution.py
+++ b/solution.py
@@ -124,19 +124,36 @@
             here = piece(strips, u, x, y)
             remote(here, here, scat_s.at[u, 0], scat_r.at[u], x, y, z, 1 - core).wait_recv()
 
+    def at(u, px, py, rows):
+        p, cols = units[u]
+        return strips.at[p, px, py, rows, cols]
+
+    for _ in share_steps(at, one_s, one_r, two_s, two_r):
+        yield
+
+    for u in range(NP):
+
+        @pl.when(roots[u])
+        def _():
+            for d in range(1, 16):
+                scatter(u, d).wait_send()
+
+    yield
+
+
+def share_steps(ref_at, one_s, one_r, two_s, two_r):
+    x, y, z, core = place()
+    every = [(order, u) for u in range(NP) for order in range(2)]
     first = []
-    for u in range(NP):
-        p, cols = units[u]
-        for order in range(2):
-            for d in range(1, 4):
-                here = strips.at[p, x, y, ROWS[order], cols]
-                tx, ty = line(order, x, y, d)
-                first.append(
-                    remote(
-                        here, here, one_s.at[order, u, d], one_r.at[order, u, d],
-                        tx, ty, z, core,
-                    )
+    for order, u in every:
+        for d in range(1, 4):
+            here = ref_at(u, x, y, ROWS[order])
+            tx, ty = line(order, x, y, d)
+            first.append(
+                remote(
+                    here, here, one_s.at[order, u, d], one_r.at[order, u, d], tx, ty, z, core
                 )
+            )
     for copy in first:
         copy.start()
     yield
@@ -145,10 +162,9 @@
         copy.wait_recv()
 
     def block(order, u, at, pick):
-        p, cols = units[u]
         if order == 0:
-            return strips.at[p, pick, (y + at) % 4, ROWS[0], cols]
-        return strips.at[p, (x + at) % 4, pick, ROWS[1], cols]
+            return ref_at(u, pick, (y + at) % 4, ROWS[0])
+        return ref_at(u, (x + at) % 4, pick, ROWS[1])
 
     def second(order, u, kind):
         whole = pl.ds(0, 4)
@@ -169,7 +185,6 @@
             ref, ref, two_s.at[order, u, kind], two_r.at[order, u, kind], x, y, z, 1 - core
         )
 
-    every = [(order, u) for u in range(NP) for order in range(2)]
     for order, u in every:
         for kind in (0, 1):
             second(order, u, kind).start()
@@ -185,13 +200,6 @@
         for kind in (2, 3):
             arrival(order, u, kind).wait_recv()
     yield
-
-    for u in range(NP):
-
-        @pl.when(roots[u])
-        def _():
-            for d in range(1, 16):
-                scatter(u, d).wait_send()
 
     for copy in first:
         copy.wait_send()
@@ -354,12 +362,35 @@
         for d in range(1, 4):
             two(order, u, d).wait_recv()
         here = y if order == 0 else x
-        fin[u, ROWS[order]] = (tot[order, u, here] + got2[order, u, 0]) + (
+        total = (tot[order, u, here] + got2[order, u, 0]) + (
             got2[order, u, 1] + got2[order, u, 2]
         )
+        if wide:
+            out[core, u, x, y, ROWS[order]] = total
+        else:
+            fin[u, ROWS[order]] = total
+
+    def sends():
+        for order, u in every:
+            for kind in range(3):
+                for way in range(2):
+                    one(order, u, kind, way).wait_send()
+            for d in range(1, 4):
+                two(order, u, d).wait_send()
+
+    if wide:
+
+        def at(u, px, py, rows):
+            return out.at[core, u, px, py, rows]
+
+        for _ in share_steps(at, *wide):
+            yield
+        sends()
+        yield
+        return
 
     def slot(u, px, py):
-        return out.at[core, u, px, py] if wide else out.at[u, px, py]
+        return out.at[u, px, py]
 
     def send(root, u):
         return remote(
@@ -374,8 +405,6 @@
             at_root = (x == 0) & (y == root)
             for u in range(NP):
                 flag = units[u][0] == root
-                if wide:
-                    flag = flag | (z == 3)
                 yield root, u, flag & at_root, flag & jnp.logical_not(at_root)
 
     for root, u, local, away in cases():
@@ -406,12 +435,7 @@
                     x, y, z, 1 - core,
                 ).wait_recv()
 
-    for order, u in every:
-        for kind in range(3):
-            for way in range(2):
-                one(order, u, kind, way).wait_send()
-        for d in range(1, 4):
-            two(order, u, d).wait_send()
+    sends()
     yield
 
 
@@ -459,7 +483,7 @@
             ref, blocks.at[core, u], ex_s.at[u], ex_r.at[u], x, y, z, 1 - core
         ).start()
         pltpu.make_async_copy(ref, blocks.at[core, u], loc.at[u]).start()
-    drive((steps, 1))
+    drive((steps, 2))
     for u in range(NP):
         p, cols = unit(0, u, core)
         ref = strips.at[p, :, :, :, cols]
@@ -501,7 +525,7 @@
     greet(with_z(*place()))
     a = along_steps(src, out, sems[7:], lax.axis_index("row") >= NP)
     s = spread_steps(1, own, strips, sems[:7])
-    drive((s, 1), (a, 1), (a, 2), (s, 1), (a, 2), (s, 1), (a, 4), (s, 1), (a, 2), (a, 1), (s, 2))
+    drive((s, 1), (a, 1), (a, 2), (s, 1), (a, 2), (s, 1), (a, 4), (s, 1), (a, 2), (a, 1), (s, 3))
 
 
 def along_spread(half, factor, strips):
@@ -525,16 +549,16 @@
     greet(plane_and_peer(x, y, z, core))
     bufs, sems = rest[:5], rest[5:]
     ex_s, ex_r = sems[-2:]
-    steps = reduce_steps(0, True, src, out, bufs, sems[:7])
-    drive((steps, 5))
-
-    @pl.when((x == 0) & (y < NP) & (z == 3))
-    def _():
+    steps = reduce_steps(0, sems[7:11], src, out, bufs, sems[:7])
+    drive((steps, 7))
+    for u in range(NP):
         remote(
-            out.at[core], out.at[core], ex_s.at[0], ex_r.at[0], x, y, z, 1 - core
+            out.at[core, u], out.at[core, u], ex_s.at[u], ex_r.at[u], x, y, z, 1 - core
         ).start()
+    drive((steps, 2))
+    for u in range(NP):
         remote(
-            out.at[core], out.at[1 - core], ex_s.at[0], ex_r.at[0], x, y, z, 1 - core
+            out.at[core, u], out.at[1 - core, u], ex_s.at[u], ex_r.at[u], x, y, z, 1 - core
         ).wait()
 
 
@@ -544,7 +568,7 @@
         out_shape=jax.ShapeDtypeStruct((2, 3, 4, 4, 32, NB), F32),
         in_specs=[VM],
         out_specs=VM,
-        scratch_shapes=REDUCE_BUFS + REDUCE_SEMS + [DMA((1,)), DMA((1,))],
+        scratch_shapes=REDUCE_BUFS + REDUCE_SEMS + [DMA((2, 3, 4))] * 4 + [DMA((3,)), DMA((3,))],
         compiler_params=comm(2, 32),
     )(part.reshape(3, 4, 4, 32, 1024))
 
@@ -553,7 +577,7 @@
     greet(with_z(*place()))
     bufs, sems = rest[:5], rest[5:]
     a = along_steps(src, out, sems[7:], lax.axis_index("row") < NP)
-    r = reduce_steps(1, False, part, rest_out, bufs, sems[:7])
+    r = reduce_steps(1, None, part, rest_out, bufs, sems[:7])
     drive((a, 1), (r, 1), (a, 3), (r, 1), (a, 3), (r, 1), (a, 1), (r, 1), (a, 3), (a, 1), (r, 1))
 
 
@@ -625,23 +649,29 @@
 def plan():
     rows = []
     l00, l10, l20, l11, l21, l22, t00, t10, t20, t11, t21, t22, i0, i1, i2 = range(15)
-    w, p, q, a2, y2, s21, s21t, a1, y1, s20, s10, s20t, s10t, a0, y0 = range(15, 30)
-
-    def mm(a, b, to, tril=0, half=0):
-        rows.append((0, a, b, to, to, tril, 0, 1, half))
+    w, p, q, a2, y2, s21, s21t, a1, y1, s20, s10, s20t, s10t, a0, y0, none = range(15, 31)
+
+    def mm(a, b, to):
+        rows.append((0, a, b, none, to, 1))
 
     def take(a, b, to):
-        rows.append((0, a, b, to, to, 0, 1, -1, 0))
+        rows.append((0, a, b, to, to, -1))
 
     def turn(a, to, add=0):
-        rows.append((1, a, a, a, to, 0, add, 1, 0))
+        rows.append((1, a, a, a, to, add))
+
+    def lower(a, twice):
+        rows.append((2, a, a, a, a, twice))
 
     def adjoint(l, i, t, a, y):
         turn(l, w)
-        mm(w, t, p, tril=1, half=1)
+        lower(t, 2)
+        mm(w, t, p)
+        lower(p, 1)
         turn(i, w)
         mm(w, p, q)
-        mm(q, i, a, half=1)
+        mm(q, i, a)
+        lower(a, 1)
         turn(a, y, add=1)
 
     adjoint(l22, i2, t22, a2, y2)
@@ -667,7 +697,7 @@
 
 
 PLAN, PICKS = plan()
-BLK = 256
+BLK = 512
 
 
 def chain_kernel(plan_ref, pick_ref, l_ref, t_ref, i_ref, q_ref, z_ref, m, high, low):
@@ -677,49 +707,50 @@
         m[6 + n] = t_ref[n]
     for n in range(3):
         m[12 + n] = i_ref[n]
+    m[30] = jnp.zeros((NB, NB), F32)
 
     def op(n, carry):
-        kind, a, b, c = (plan_ref[n, j] for j in range(4))
-        to, tril, keep, sign, half = (plan_ref[n, j] for j in range(4, 9))
+        kind, a, b, c, to, value = (plan_ref[n, j] for j in range(6))
+        scale = value.astype(F32)
 
         @pl.when(kind == 0)
         def _():
             def split(i, carry):
+                at = pl.ds(pl.multiple_of(i * 128, 128), 128)
+                own = m[b, at]
+                top = own.astype(jnp.bfloat16)
+                high[0, at] = top
+                high[1, at] = (own - top.astype(F32)).astype(jnp.bfloat16)
+                high[2, at] = top
+                own = m[a, at] * scale
+                top = own.astype(jnp.bfloat16)
+                low[at, :NB] = top
+                low[at, NB : 2 * NB] = top
+                low[at, 2 * NB :] = (own - top.astype(F32)).astype(jnp.bfloat16)
+                return carry
+
+            lax.fori_loop(0, 4, split, 0)
+            right = high[...].reshape(3 * NB, NB)
+            m[to] = m[c] + jnp.dot(low[...], right, preferred_element_type=F32)
+
+        @pl.when(kind == 2)
+        def _():
+            def mask(i, carry):
                 at = pl.ds(pl.multiple_of(i * 128, 128), 128)
                 rows = lax.broadcasted_iota(jnp.int32, (128, NB), 0) + i * 128
                 cols = lax.broadcasted_iota(jnp.int32, (128, NB), 1)
-                value = jnp.where((cols - rows) * tril > 0, 0.0, m[b, at])
-                top = value.astype(jnp.bfloat16)
-                high[at] = top
-                low[at] = (value - top.astype(F32)).astype(jnp.bfloat16)
+                own = m[a, at]
+                diag = jnp.where(rows == cols, own * (0.5 * scale), 0.0)
+                m[to, at] = jnp.where(rows > cols, own, diag)
                 return carry
 
-            lax.fori_loop(0, 4, split, 0)
-
-            def product(i, carry):
-                at = pl.ds(pl.multiple_of(i * BLK, BLK), BLK)
-                value = m[a, at]
-                top = value.astype(jnp.bfloat16)
-                rest = (value - top.astype(F32)).astype(jnp.bfloat16)
-                right = high[...]
-                total = jnp.dot(rest, right, preferred_element_type=F32)
-                total += jnp.dot(top, low[...], preferred_element_type=F32)
-                total += jnp.dot(top, right, preferred_element_type=F32)
-                rows = lax.broadcasted_iota(jnp.int32, (BLK, NB), 0) + i * BLK
-                cols = lax.broadcasted_iota(jnp.int32, (BLK, NB), 1)
-                total = total * sign.astype(F32)
-                halved = jnp.where(rows > cols, total, jnp.where(rows == cols, 0.5 * total, 0.0))
-                total = jnp.where(half > 0, halved, total)
-                m[to, at] = jnp.where(keep > 0, m[c, at], 0.0) + total
-                return carry
-
-            lax.fori_loop(0, NB // BLK, product, 0)
+            lax.fori_loop(0, 4, mask, 0)
 
         @pl.when(kind == 1)
         def _():
             def turn(i, carry):
                 at = pl.ds(pl.multiple_of(i * 128, 128), 128)
-                m[to, :, at] = m[a, at].T + jnp.where(keep > 0, m[a, :, at], 0.0)
+                m[to, :, at] = m[a, at].T + m[a, :, at] * scale
                 return carry
 
             lax.fori_loop(0, 4, turn, 0)
@@ -745,11 +776,11 @@
         in_specs=[smem, smem, VM, VM, VM],
         out_specs=(VM, VM),
         scratch_shapes=[
-            pltpu.VMEM((30, NB, NB), F32),
-            pltpu.VMEM((NB, NB), jnp.bfloat16),
-            pltpu.VMEM((NB, NB), jnp.bfloat16),
+            pltpu.VMEM((31, NB, NB), F32),
+            pltpu.VMEM((3, NB, NB), jnp.bfloat16),
+            pltpu.VMEM((NB, 3 * NB), jnp.bfloat16),
         ],
-        compiler_params=pltpu.CompilerParams(vmem_limit_bytes=56 << 20),
+        compiler_params=pltpu.CompilerParams(vmem_limit_bytes=58 << 20),
     )(jnp.array(PLAN, jnp.int32), jnp.array(PICKS, jnp.int32), blocks, near, inv)
 
 

time: 317 us -> 300 us (0.946)
  Pallas kernels: 292 us -> 278 us
  local copies, waits for them, and re-layouts: 13.7 us -> 10.3 us
    pallas_call x1, Pallas kernels: 74.8 us -> 52 us  [along_reduce(): pl.pallas_call(along_reduce_kernel, out_shape=(jax.ShapeDtypeStruct((2, 2...]
    pallas_call x1, Pallas kernels: 39.4 us -> 52.9 us  [reduce_rows(): pl.pallas_call(reduce_kernel, out_shape=jax.ShapeDtypeStruct((2, 3, 4, 4,...]
    pallas_call x1, Pallas kernels: 49.7 us -> 46.2 us  [chain(): pl.pallas_call(chain_kernel, out_shape=(jax.ShapeDtypeStruct((256, 3 * NB...]
    unnamed x26 -> x20, local copies, waits for them, and re-layouts: 13.4 us -> 9.97 us
where the time goes in v2:
time: 300 us
  Pallas kernels  278 us (93%)
  local copies, waits for them, and re-layouts  10.3 us (3%)
  matrix products  8.93 us (3%)
    pallas_call x1, Pallas kernels, reduce_rows(): pl.pallas_call(reduce_kernel, out_shape=jax.ShapeDtypeStruct((2, 3, 4, 4,...  52.9 us
    pallas_call x1, Pallas kernels, along_reduce(): pl.pallas_call(along_reduce_kernel, out_shape=(jax.ShapeDtypeStruct((2, 2...  52 us
    pallas_call x1, Pallas kernels, spread(): pl.pallas_call(spread_kernel, out_shape=(jax.ShapeDtypeStruct((3, 4, 4, 3...  49.9 us
    pallas_call x1, Pallas kernels, along_spread(): pl.pallas_call(along_spread_kernel, out_shape=(jax.ShapeDtypeStruct((2, 2...  48.1 us
    pallas_call x1, Pallas kernels, chain(): pl.pallas_call(chain_kernel, out_shape=(jax.ShapeDtypeStruct((256, 3 * NB...  46.2 us
    pallas_call x1, Pallas kernels, finish(): pl.pallas_call(finish_kernel, out_shape=jax.ShapeDtypeStruct((NB, 2 * NB)...  14.7 us
    pallas_call x1, Pallas kernels, invert(): pl.pallas_call(invert_kernel, out_shape=jax.ShapeDtypeStruct((NP, NB, NB)...  14.4 us
    unnamed x20, local copies, waits for them, and re-layouts  9.97 us

profile of v2, /device:TPU:1, one launch (start us, length us, event | category | flops | bytes accessed | tf_op | source)
XLA Modules:
  0.0 299.8 jit_solution(30029921061455576)
XLA Ops:
  0.0 1.6 copy-done.3
  1.6 1.6 copy-done.8
  3.2 49.9 %shard_map.46 = (f32[3,4,4,32,1024]{4,3,2,1,0:T(8,128)S(1)}, f32[2,3,4,4,32,512]{5,4,3,2,1,0:T(8,128)S(1)}, f32[256,1024]{1,0:T(8,128)S(1)}) custom-call(f32[4,4,32,1024]{3,2,1,0:T(8,128)S(1)} %bitcast.55, f32[512,1024]{1,0:T(8,128)S(1)} %copy-done.3), custom_call_target="tpu_custom_call" | custom-call | tf_op jit(solution)/shard_map/pallas_call | solution.py:504
  53.1 0.1 dynamic-slice_select_fusion
  53.3 0.3 slice_bitcast_fusion.14
  53.6 0.3 pad_maximum_fusion.d_ref
  53.9 14.4 %shard_map.47.i_ref = f32[3,512,512]{2,1,0:T(8,128)S(1)} custom-call(f32[3,512,512]{2,1,0:T(8,128)S(1)} %pad_maximum_fusion.d_ref), custom_call_target="tpu_custom_call" | custom-call | tf_op jit(solution)/shard_map/pallas_call | solution.py:640
  68.3 0.6 fusion.2
  69.0 0.6 convolution_subtract_fusion.2
  69.6 0.6 convolution_subtract_fusion.1
  70.2 0.6 fusion.1
  70.9 0.6 convolution_subtract_fusion
  71.5 0.6 fusion
  72.1 0.1 pad_maximum_fusion.1
  72.2 48.1 %shard_map.48 = (f32[2,2,8,16,1536]{4,3,2,1,0:T(8,128)S(1)}, f32[3,4,4,32,1024]{4,3,2,1,0:T(8,128)S(1)}) custom-call(f32[1,2,8,16,1536]{4,3,2,1,0:T(8,128)S(1)} %bitcast.57, f32[4,4,32,1024]{3,2,1,0:T(8,128)S(1)} %bitcast.56, f32[3,4,4,32,1024]{4,3,2,1,0:T(8,128)S(1)} %get-tuple-element.16._), custom_call_target="tpu_custom_call", output_to_operand_aliasing={{1}: (2, {})} | custom-call | tf_op jit(solution)/shard_map/pallas_call | solution.py:532
  120.4 5.2 %negate_select_fusion = f32[1536,1024]{1,0:T(8,128)S(1)} fusion(f32[512,1536]{1,0:T(8,128)S(1)} %bitcast.53, f32[512,1024]{1,0:T(8,128)S(1)} %copy-done.8, pred[]{:T(512)S(6)} %ge.3), kind=kOutput, calls=%fused_computation | convolution fusion | flops 4834983936 | bytes 11534337 | tf_op jit(solution)/shard_map/dot_general | solution.py:21
  125.6 1.7 broadcast_select_fusion.src.part
  127.3 52.9 %shard_map.49 = f32[2,3,4,4,32,512]{5,4,3,2,1,0:T(8,128)S(1)} custom-call(f32[3,4,4,32,1024]{4,3,2,1,0:T(8,128)S(1)} %broadcast_select_fusion.src.part), custom_call_target="tpu_custom_call" | custom-call | tf_op jit(solution)/shard_map/pallas_call | solution.py:566
  180.2 2.6 copy-done
  182.8 46.2 %shard_map.50 = (f32[256,1536]{1,0:T(8,128)}, f32[3,512,512]{2,1,0:T(8,128)}) custom-call(s32[41,6]{1,0:T(8,128)} %constant.35.clone.plan_ref, s32[3,6]{1,0:T(4,128)} %constant.36.clone.pick_ref, f32[6,512,512]{2,1,0:T(8,128)} %bitcast.51, f32[6,512,512]{2,1,0:T(8,128)} %bitcast.44, f32[3,512,512]{2,1,0:T(8,128)} %copy-done.5), custom_call_target="tpu_custom_call" | custom-call | tf_op jit(solution)/shard_map/pallas_call | solution.py:770
  228.9 2.8 copy-done.2
  231.7 1.4 copy-done.9
  233.1 52.0 %shard_map.51 = (f32[2,2,8,16,1536]{4,3,2,1,0:T(8,128)S(1)}, f32[3,4,4,32,512]{4,3,2,1,0:T(8,128)S(1)}) custom-call(f32[1,2,8,16,1536]{4,3,2,1,0:T(8,128)S(1)} %bitcast.60, f32[3,4,4,32,1024]{4,3,2,1,0:T(8,128)S(1)} %copy-done.2), custom_call_target="tpu_custom_call" | custom-call | tf_op jit(solution)/shard_map/pallas_call | solution.py:585
  285.1 14.7 %shard_map.52 = f32[512,1024]{1,0:T(8,128)} custom-call(f32[512,1024]{1,0:T(8,128)S(1)} %copy-done.4, f32[512,1536]{1,0:T(8,128)S(1)} %bitcast.54, f32[512,1536]{1,0:T(8,128)S(1)} %bitcast.58, f32[1536,1024]{1,0:T(8,128)} %bitcast.52, f32[3,512,512]{2,1,0:T(8,128)S(1)} %bitcast.59, f32[2,3,512,512]{3,2,1,0:T(8,128)} %bitcast.45, ...), custom_call_target="tpu_custom_call" | custom-call | tf_op jit(solution)/shard_map/pallas_call | solution.py:873
  (16 shorter events, 0.0 us)
Async XLA Ops:
  0.0 1.6 copy-start.3
  1.6 1.6 copy-start.8
  53.1 17.8 %copy-start.6 = (f32[2,3,4,4,32,512]{5,4,3,2,1,0:T(8,128)}, f32[2,3,4,4,32,512]{5,4,3,2,1,0:T(8,128)S(1)}, u32[]{:S(2)}) copy-start(f32[2,3,4,4,32,512]{5,4,3,2,1,0:T(8,128)S(1)} %get-tuple-element.15) | copy-start | bytes 18874372
  68.3 3.2 %copy-start.5 = (f32[3,512,512]{2,1,0:T(8,128)}, f32[3,512,512]{2,1,0:T(8,128)S(1)}, u32[]{:S(2)}) copy-start(f32[3,512,512]{2,1,0:T(8,128)S(1)} %shard_map.47.i_ref) | copy-start | bytes 9437188
  120.3 5.2 %copy-start.7 = (f32[3,4,4,32,1024]{4,3,2,1,0:T(8,128)}, f32[3,4,4,32,1024]{4,3,2,1,0:T(8,128)S(1)}, u32[]{:S(2)}) copy-start(f32[3,4,4,32,1024]{4,3,2,1,0:T(8,128)S(1)} %get-tuple-element.20) | copy-start | bytes 18874372
  120.3 5.2 %copy-start.4 = (f32[512,1024]{1,0:T(8,128)S(1)}, f32[512,1024]{1,0:T(8,128)}, u32[]{:S(2)}) copy-start(f32[512,1024]{1,0:T(8,128)} %cot.3) | copy-start | bytes 6291460
  127.3 52.9 %copy-start.1 = (f32[3,4,4,32,1024]{4,3,2,1,0:T(8,128)}, f32[3,4,4,32,1024]{4,3,2,1,0:T(8,128)S(1)}, u32[]{:S(2)}) copy-start(f32[3,4,4,32,1024]{4,3,2,1,0:T(8,128)S(1)} %broadcast_select_fusion.src.part) | copy-start | bytes 18874372
  180.2 2.6 copy-start
  228.9 2.8 copy-start.2
  231.7 1.4 copy-start.9

commit v3 on v2

--- a/solution.py
+++ b/solution.py
@@ -81,7 +81,7 @@
     return ((x + d) % 4, y) if order == 0 else (x, (y + d) % 4)
 
 
-def spread_steps(part, own, strips, sems):
+def spread_steps(part, own, strips, sems, hand=None):
     scat_s, scat_r, one_s, one_r, two_s, two_r, loc = sems
     x, y, z, core = place()
     units = [unit(part, u, core) for u in range(NP)]
@@ -128,7 +128,7 @@
         p, cols = units[u]
         return strips.at[p, px, py, rows, cols]
 
-    for _ in share_steps(at, one_s, one_r, two_s, two_r):
+    for _ in share_steps(at, one_s, one_r, two_s, two_r, hand):
         yield
 
     for u in range(NP):
@@ -141,7 +141,16 @@
     yield
 
 
-def share_steps(ref_at, one_s, one_r, two_s, two_r):
+def piece_line(order, x, y, at):
+    if order == 0:
+        return pl.ds(0, 4), (y + at) % 4, ROWS[0]
+    return (x + at) % 4, pl.ds(0, 4), ROWS[1]
+
+
+ALL_LINES = [(order, u, at) for order in range(2) for u in range(NP) for at in range(4)]
+
+
+def share_steps(ref_at, one_s, one_r, two_s, two_r, hand=None):
     x, y, z, core = place()
     every = [(order, u) for u in range(NP) for order in range(2)]
     first = []
@@ -185,20 +194,30 @@
             ref, ref, two_s.at[order, u, kind], two_r.at[order, u, kind], x, y, z, 1 - core
         )
 
+    whole_line = pl.ds(0, 4)
     for order, u in every:
         for kind in (0, 1):
             second(order, u, kind).start()
+    if hand:
+        for order, u in every:
+            hand(order, u, 0, block(order, u, 0, whole_line))
     yield
 
     for order, u in every:
         for kind in (0, 1):
             arrival(order, u, kind).wait_recv()
             second(order, u, kind + 2).start()
+    if hand:
+        for order, u in every:
+            for at in (3, 1):
+                hand(order, u, at, block(order, u, at, whole_line))
     yield
 
     for order, u in every:
         for kind in (2, 3):
             arrival(order, u, kind).wait_recv()
+        if hand:
+            hand(order, u, 2, block(order, u, 2, whole_line))
     yield
 
     for copy in first:
@@ -293,7 +312,7 @@
     yield
 
 
-def reduce_steps(part, wide, src, out, bufs, sems):
+def reduce_steps(part, wide, src, out, bufs, sems, hand=None):
     got, acc, tot, got2, fin = bufs
     one_s, one_r, two_s, two_r, g_s, g_r, loc = sems
     x, y, z, core = place()
@@ -383,7 +402,7 @@
         def at(u, px, py, rows):
             return out.at[core, u, px, py, rows]
 
-        for _ in share_steps(at, *wide):
+        for _ in share_steps(at, *wide, hand):
             yield
         sends()
         yield
@@ -469,28 +488,34 @@
 def spread_kernel(own, cot, strips, blocks, half, *sems):
     x, y, z, core = place()
     greet(plane_and_peer(x, y, z, core))
-    ex_s, ex_r, loc = sems[-3:]
+    ex_s, ex_r, loc, half_s, half_r = sems[-5:]
     half_copy = remote(
-        cot.at[pl.ds(256 * (1 - core), 256)], half, ex_s.at[3], ex_r.at[3], x, y, z, 1 - core
+        cot.at[pl.ds(256 * (1 - core), 256)], half, half_s.at[0], half_r.at[0], x, y, z, 1 - core
     )
     half_copy.start()
-    steps = spread_steps(0, own, strips, sems[:7])
-    drive((steps, 5))
-    for u in range(NP):
+    def over(order, u, at, ref):
+        px, py, rows = piece_line(order, x, y, at)
+        there = blocks.at[core, u, px, py, rows]
+        return (
+            remote(ref, there, ex_s.at[order, u, at], ex_r.at[order, u, at], x, y, z, 1 - core),
+            pltpu.make_async_copy(ref, there, loc.at[order, u, at]),
+        )
+
+    def hand(order, u, at, ref):
+        for copy in over(order, u, at, ref):
+            copy.start()
+
+    drive((spread_steps(0, own, strips, sems[:7], hand), 7))
+    for order, u, at in ALL_LINES:
+        px, py, rows = piece_line(order, x, y, at)
         p, cols = unit(0, u, core)
-        ref = strips.at[p, :, :, :, cols]
+        away, here = over(order, u, at, strips.at[p, px, py, rows, cols])
+        here.wait()
+        away.wait_send()
+        got = blocks.at[1 - core, u, px, py, rows]
         remote(
-            ref, blocks.at[core, u], ex_s.at[u], ex_r.at[u], x, y, z, 1 - core
-        ).start()
-        pltpu.make_async_copy(ref, blocks.at[core, u], loc.at[u]).start()
-    drive((steps, 2))
-    for u in range(NP):
-        p, cols = unit(0, u, core)
-        ref = strips.at[p, :, :, :, cols]
-        pltpu.make_async_copy(ref, blocks.at[core, u], loc.at[u]).wait()
-        remote(
-            ref, blocks.at[1 - core, u], ex_s.at[u], ex_r.at[u], x, y, z, 1 - core
-        ).wait()
+            got, got, ex_s.at[order, u, at], ex_r.at[order, u, at], x, y, z, 1 - core
+        ).wait_recv()
     half_copy.wait()
 
 
@@ -510,8 +535,8 @@
         ),
         in_specs=[ANY, ANY],
         out_specs=(ANY, VM, VM),
-        scratch_shapes=SPREAD_SEMS + [DMA((4,)), DMA((4,)), DMA((3,))],
-        compiler_params=comm(0, 32),
+        scratch_shapes=SPREAD_SEMS + [DMA((2, 3, 4))] * 3 + [DMA((1,)), DMA((1,))],
+        compiler_params=comm(0, 60),
     )(factor.reshape(4, 4, 32, 1024), cot)
 
 
@@ -539,7 +564,7 @@
         out_specs=(VM, ANY),
         scratch_shapes=SPREAD_SEMS + ALONG_SEMS,
         input_output_aliases={2: 1},
-        compiler_params=comm(1, 16),
+        compiler_params=comm(1, 60),
     )(half.reshape(1, 2, CH, CR, 1536), factor.reshape(4, 4, 32, 1024), strips)
     return out.reshape(512, 1536), strips.reshape(1536, 1024)
 
@@ -549,17 +574,20 @@
     greet(plane_and_peer(x, y, z, core))
     bufs, sems = rest[:5], rest[5:]
     ex_s, ex_r = sems[-2:]
-    steps = reduce_steps(0, sems[7:11], src, out, bufs, sems[:7])
-    drive((steps, 7))
-    for u in range(NP):
-        remote(
-            out.at[core, u], out.at[core, u], ex_s.at[u], ex_r.at[u], x, y, z, 1 - core
-        ).start()
-    drive((steps, 2))
-    for u in range(NP):
-        remote(
-            out.at[core, u], out.at[1 - core, u], ex_s.at[u], ex_r.at[u], x, y, z, 1 - core
-        ).wait()
+
+    def over(order, u, at, ref):
+        return remote(
+            ref, ref, ex_s.at[order, u, at], ex_r.at[order, u, at], x, y, z, 1 - core
+        )
+
+    def hand(order, u, at, ref):
+        over(order, u, at, ref).start()
+
+    drive((reduce_steps(0, sems[7:11], src, out, bufs, sems[:7], hand), 9))
+    for order, u, at in ALL_LINES:
+        px, py, rows = piece_line(order, x, y, at)
+        over(order, u, at, out.at[core, u, px, py, rows]).wait_send()
+        over(order, u, at, out.at[1 - core, u, px, py, rows]).wait_recv()
 
 
 def reduce_rows(part):
@@ -568,7 +596,7 @@
         out_shape=jax.ShapeDtypeStruct((2, 3, 4, 4, 32, NB), F32),
         in_specs=[VM],
         out_specs=VM,
-        scratch_shapes=REDUCE_BUFS + REDUCE_SEMS + [DMA((2, 3, 4))] * 4 + [DMA((3,)), DMA((3,))],
+        scratch_shapes=REDUCE_BUFS + REDUCE_SEMS + [DMA((2, 3, 4))] * 6,
         compiler_params=comm(2, 32),
     )(part.reshape(3, 4, 4, 32, 1024))
 
@@ -780,7 +808,7 @@
             pltpu.VMEM((3, NB, NB), jnp.bfloat16),
             pltpu.VMEM((NB, 3 * NB), jnp.bfloat16),
         ],
-        compiler_params=pltpu.CompilerParams(vmem_limit_bytes=58 << 20),
+        compiler_params=pltpu.CompilerParams(vmem_limit_bytes=55 << 20),
     )(jnp.array(PLAN, jnp.int32), jnp.array(PICKS, jnp.int32), blocks, near, inv)
 
 

time: 300 us -> 299 us (level)
  local copies, waits for them, and re-layouts: 10.3 us -> 6.18 us
    unnamed x20 -> x16, local copies, waits for them, and re-layouts: 9.97 us -> 4.01 us
    pallas_call x1, Pallas kernels: 52.9 us -> 47.8 us  [reduce_rows(): pl.pallas_call(reduce_kernel, out_shape=jax.ShapeDtypeStruct((2, 3, 4, 4,...]
    pallas_call x1, Pallas kernels: 48.1 us -> 51.9 us  [along_spread(): pl.pallas_call(along_spread_kernel, out_shape=(jax.ShapeDtypeStruct((2, 2...]
where the time goes in v3:
time: 299 us; the launch traced here: 298 us
  Pallas kernels  278 us (93%)
  matrix products  11.6 us (4%)
  local copies, waits for them, and re-layouts  6.18 us (2%)
    pallas_call x1, Pallas kernels, along_reduce(): pl.pallas_call(along_reduce_kernel, out_shape=(jax.ShapeDtypeStruct((2, 2...  52 us
    pallas_call x1, Pallas kernels, along_spread(): pl.pallas_call(along_spread_kernel, out_shape=(jax.ShapeDtypeStruct((2, 2...  51.9 us
    pallas_call x1, Pallas kernels, spread(): pl.pallas_call(spread_kernel, out_shape=(jax.ShapeDtypeStruct((3, 4, 4, 3...  50.8 us
    pallas_call x1, Pallas kernels, reduce_rows(): pl.pallas_call(reduce_kernel, out_shape=jax.ShapeDtypeStruct((2, 3, 4, 4,...  47.8 us
    pallas_call x1, Pallas kernels, chain(): pl.pallas_call(chain_kernel, out_shape=(jax.ShapeDtypeStruct((256, 3 * NB...  46.2 us
    pallas_call x1, Pallas kernels, finish(): pl.pallas_call(finish_kernel, out_shape=jax.ShapeDtypeStruct((NB, 2 * NB)...  14.7 us
    pallas_call x1, Pallas kernels, invert(): pl.pallas_call(invert_kernel, out_shape=jax.ShapeDtypeStruct((NP, NB, NB)...  14.4 us
    dot_general x1, matrix products, dot_t(): lax.dot_general(a, b, (((0,), (0,)), ((), ())), precision=precision, pref...  7.74 us

profile of v3, /device:TPU:1, one launch (start us, length us, event | category | flops | bytes accessed | tf_op | source)
XLA Modules:
  0.0 298.5 jit_solution(2443069251091438785)
XLA Ops:
  0.0 50.8 %shard_map.46 = (f32[3,4,4,32,1024]{4,3,2,1,0:T(8,128)}, f32[2,3,4,4,32,512]{5,4,3,2,1,0:T(8,128)}, f32[256,1024]{1,0:T(8,128)}) custom-call(f32[4,4,32,1024]{3,2,1,0:T(8,128)} %bitcast.61, f32[512,1024]{1,0:T(8,128)} %cot.3), custom_call_target="tpu_custom_call" | custom-call | tf_op jit(solution)/shard_map/pallas_call | solution.py:529
  50.8 0.2 dynamic-slice_select_fusion
  51.0 2.2 slice_bitcast_fusion.14
  53.2 0.0 slice-start
  53.2 0.3 pad_maximum_fusion.d_ref
  53.5 0.0 slice-start.1
  53.5 0.0 copy-start.5
  53.5 14.4 %shard_map.47.i_ref = f32[3,512,512]{2,1,0:T(8,128)S(1)} custom-call(f32[3,512,512]{2,1,0:T(8,128)S(1)} %pad_maximum_fusion.d_ref), custom_call_target="tpu_custom_call" | custom-call | tf_op jit(solution)/shard_map/pallas_call | solution.py:668
  67.9 0.6 fusion.2
  68.6 0.7 convolution_subtract_fusion.2
  69.3 0.7 convolution_subtract_fusion.1
  69.9 0.6 fusion.1
  70.6 0.6 convolution_subtract_fusion
  71.2 0.6 fusion
  71.8 1.3 pad_maximum_fusion.1
  73.1 51.9 %shard_map.48 = (f32[2,2,8,16,1536]{4,3,2,1,0:T(8,128)}, f32[3,4,4,32,1024]{4,3,2,1,0:T(8,128)}) custom-call(f32[1,2,8,16,1536]{4,3,2,1,0:T(8,128)} %bitcast.63, f32[4,4,32,1024]{3,2,1,0:T(8,128)} %bitcast.62, f32[3,4,4,32,1024]{4,3,2,1,0:T(8,128)} %get-tuple-element.16._), custom_call_target="tpu_custom_call", output_to_operand_aliasing={{1}: (2, {})} | custom-call | tf_op jit(solution)/shard_map/pallas_call | solution.py:557
  125.0 7.7 %negate_select_fusion = f32[1536,1024]{1,0:T(8,128)S(1)} fusion(f32[512,1536]{1,0:T(8,128)} %bitcast.47, f32[512,1024]{1,0:T(8,128)} %param.4, pred[]{:T(512)S(6)} %ge.3), kind=kOutput, calls=%fused_computation | convolution fusion | flops 4834983936 | bytes 11534337 | tf_op jit(solution)/shard_map/dot_general | solution.py:21
  132.7 1.0 broadcast_select_fusion.src.part
  133.7 47.8 %shard_map.49 = f32[2,3,4,4,32,512]{5,4,3,2,1,0:T(8,128)S(1)} custom-call(f32[3,4,4,32,1024]{4,3,2,1,0:T(8,128)S(1)} %broadcast_select_fusion.src.part), custom_call_target="tpu_custom_call" | custom-call | tf_op jit(solution)/shard_map/pallas_call | solution.py:594
  181.6 2.6 copy-done
  184.2 46.2 %shard_map.50 = (f32[256,1536]{1,0:T(8,128)}, f32[3,512,512]{2,1,0:T(8,128)}) custom-call(s32[41,6]{1,0:T(8,128)} %constant.35.clone.plan_ref, s32[3,6]{1,0:T(4,128)} %constant.36.clone.pick_ref, f32[6,512,512]{2,1,0:T(8,128)} %bitcast.54, f32[6,512,512]{2,1,0:T(8,128)} %bitcast.44, f32[3,512,512]{2,1,0:T(8,128)} %copy-done.2), custom_call_target="tpu_custom_call" | custom-call | tf_op jit(solution)/shard_map/pallas_call | solution.py:798
  230.3 1.4 copy-done.4
  231.7 52.0 %shard_map.51 = (f32[2,2,8,16,1536]{4,3,2,1,0:T(8,128)S(1)}, f32[3,4,4,32,512]{4,3,2,1,0:T(8,128)S(1)}) custom-call(f32[1,2,8,16,1536]{4,3,2,1,0:T(8,128)S(1)} %bitcast.51, f32[3,4,4,32,1024]{4,3,2,1,0:T(8,128)S(1)} %broadcast_select_fusion.src.part), custom_call_target="tpu_custom_call" | custom-call | tf_op jit(solution)/shard_map/pallas_call | solution.py:613
  283.8 14.7 %shard_map.52 = f32[512,1024]{1,0:T(8,128)} custom-call(f32[512,1024]{1,0:T(8,128)S(1)} %copy-done.1, f32[512,1536]{1,0:T(8,128)S(1)} %bitcast.48, f32[512,1536]{1,0:T(8,128)S(1)} %bitcast.49, f32[1536,1024]{1,0:T(8,128)} %bitcast.60, f32[3,512,512]{2,1,0:T(8,128)S(1)} %bitcast.50, f32[2,3,512,512]{3,2,1,0:T(8,128)} %bitcast.45, ...), custom_call_target="tpu_custom_call" | custom-call | tf_op jit(solution)/shard_map/pallas_call | solution.py:901
  (13 shorter events, 0.0 us)
Async XLA Ops:
  0.0 50.8 %copy-start.1 = (f32[512,1024]{1,0:T(8,128)S(1)}, f32[512,1024]{1,0:T(8,128)}, u32[]{:S(2)}) copy-start(f32[512,1024]{1,0:T(8,128)} %cot.3) | copy-start | bytes 6291460
  53.2 15.4 %slice-start = ((s8[6291456]{0:T(1024)(128)(4,1)}), s8[4194304]{0:T(1024)(128)(4,1)S(1)}, s32[]{:S(2)}) async-start(s8[6291456]{0:T(1024)(128)(4,1)} %bitcast.55), calls=%async_computation | async-start | bytes 8388608
  53.5 15.1 %slice-start.1 = ((s8[6291456]{0:T(1024)(128)(4,1)}), s8[2097152]{0:T(1024)(128)(4,1)S(1)}, s32[]{:S(2)}) async-start(s8[6291456]{0:T(1024)(128)(4,1)} %bitcast.55), calls=%async_computation.1 | async-start | bytes 4194304
  53.5 15.1 %copy-start.5 = (f32[256,1024]{1,0:T(8,128)S(1)}, f32[256,1024]{1,0:T(8,128)}, u32[]{:S(2)}) copy-start(f32[256,1024]{1,0:T(8,128)} %get-tuple-element.14) | copy-start | bytes 3145732
  67.9 3.3 %copy-start.2 = (f32[3,512,512]{2,1,0:T(8,128)}, f32[3,512,512]{2,1,0:T(8,128)S(1)}, u32[]{:S(2)}) copy-start(f32[3,512,512]{2,1,0:T(8,128)S(1)} %shard_map.47.i_ref) | copy-start | bytes 9437188
  181.6 2.6 copy-start
  230.3 1.4 copy-start.4
  231.7 52.1 %copy-start.3 = (f32[2,2,8,16,1536]{4,3,2,1,0:T(8,128)S(1)}, f32[2,2,8,16,1536]{4,3,2,1,0:T(8,128)}, u32[]{:S(2)}) copy-start(f32[2,2,8,16,1536]{4,3,2,1,0:T(8,128)} %get-tuple-element.17) | copy-start | bytes 9437188

commit v4 on v3

--- a/solution.py
+++ b/solution.py
@@ -228,7 +228,7 @@
     yield
 
 
-AHEAD = 3
+AHEAD = 5
 
 
 def along_steps(src, out, sems, used):
@@ -387,7 +387,7 @@
         if wide:
             out[core, u, x, y, ROWS[order]] = total
         else:
-            fin[u, ROWS[order]] = total
+            fin[order, u, x if order == 0 else y] = total
 
     def sends():
         for order, u in every:
@@ -408,50 +408,85 @@
         yield
         return
 
-    def slot(u, px, py):
-        return out.at[u, px, py]
-
-    def send(root, u):
+    def to_line(order, u):
+        mine = fin.at[order, u, x if order == 0 else y]
+        target = (0, y) if order == 0 else (x, units[u][0])
         return remote(
-            fin.at[u], slot(u, x, y), g_s.at[root, u], g_r.at[u, x * 4 + y], 0, root, z, core
-        )
-
-    def keep(u):
-        return pltpu.make_async_copy(fin.at[u], slot(u, x, y), loc.at[u])
-
-    def cases():
-        for root in range(NP):
-            at_root = (x == 0) & (y == root)
-            for u in range(NP):
-                flag = units[u][0] == root
-                yield root, u, flag & at_root, flag & jnp.logical_not(at_root)
-
-    for root, u, local, away in cases():
-
-        @pl.when(away)
-        def _():
-            send(root, u).start()
-
-        @pl.when(local)
-        def _():
-            keep(u).start()
-
-    yield
-
-    for root, u, local, away in cases():
-
-        @pl.when(away)
-        def _():
-            send(root, u).wait_send()
-
-        @pl.when(local)
-        def _():
-            keep(u).wait()
-            for d in range(1, 16):
-                sx, sy = (x + d // 4) % 4, (y + d % 4) % 4
+            mine, mine, g_s.at[0, order, u], g_r.at[0, order, u, x if order == 0 else y],
+            *target, z, core,
+        )
+
+    def target_lines(order, u, px, py):
+        if order == 0:
+            return out.at[u, pl.ds(0, 4), py, ROWS[0]]
+        return out.at[u, px, pl.ds(0, 4), ROWS[1]]
+
+    def to_root(order, u):
+        return remote(
+            fin.at[order, u], target_lines(order, u, x, y), g_s.at[1, order, u],
+            g_r.at[1, order, u, y if order == 0 else x], 0, units[u][0], z, core,
+        )
+
+    def keep(order, u):
+        return pltpu.make_async_copy(
+            fin.at[order, u], target_lines(order, u, x, y), loc.at[order, u]
+        )
+
+    def on_line(order, u):
+        return x == 0 if order == 0 else y == units[u][0]
+
+    def at_root(u):
+        return (x == 0) & (y == units[u][0])
+
+    for order, u in every:
+
+        @pl.when(jnp.logical_not(on_line(order, u)))
+        def _():
+            to_line(order, u).start()
+
+    yield
+
+    for order, u in every:
+
+        @pl.when(on_line(order, u))
+        def _():
+            for d in range(1, 4):
+                index = ((x if order == 0 else y) + d) % 4
+                here = fin.at[order, u, index]
                 remote(
-                    fin.at[u], slot(u, sx, sy), g_s.at[root, u], g_r.at[u, sx * 4 + sy],
+                    here, here, g_s.at[0, order, u], g_r.at[0, order, u, index],
                     x, y, z, 1 - core,
+                ).wait_recv()
+
+        @pl.when(on_line(order, u) & jnp.logical_not(at_root(u)))
+        def _():
+            to_root(order, u).start()
+
+        @pl.when(at_root(u))
+        def _():
+            keep(order, u).start()
+
+    yield
+
+    for order, u in every:
+
+        @pl.when(jnp.logical_not(on_line(order, u)))
+        def _():
+            to_line(order, u).wait_send()
+
+        @pl.when(on_line(order, u) & jnp.logical_not(at_root(u)))
+        def _():
+            to_root(order, u).wait_send()
+
+        @pl.when(at_root(u))
+        def _():
+            keep(order, u).wait()
+            for d in range(1, 4):
+                px, py = (x + d) % 4, (y + d) % 4
+                there = target_lines(order, u, px, py)
+                remote(
+                    there, there, g_s.at[1, order, u],
+                    g_r.at[1, order, u, py if order == 0 else px], x, y, z, 1 - core,
                 ).wait_recv()
 
     sends()
@@ -469,11 +504,11 @@
     pltpu.VMEM((2, 3, 2, 2, 16, NB), F32),
     pltpu.VMEM((2, 3, 4, 16, NB), F32),
     pltpu.VMEM((2, 3, 3, 16, NB), F32),
-    pltpu.VMEM((3, 32, NB), F32),
+    pltpu.VMEM((2, 3, 4, 16, NB), F32),
 ]
 REDUCE_SEMS = [
-    DMA((2, 3, 6)), DMA((2, 3, 6)), DMA((2, 3, 4)), DMA((2, 3, 4)), DMA((3, 3)), DMA((3, 16)),
-    DMA((3,)),
+    DMA((2, 3, 6)), DMA((2, 3, 6)), DMA((2, 3, 4)), DMA((2, 3, 4)), DMA((2, 2, 3)), DMA((2, 2, 3, 4)),
+    DMA((2, 3)),
 ]
 VM = pl.BlockSpec(memory_space=pltpu.VMEM)
 ANY = pl.BlockSpec(memory_space=pl.ANY)
@@ -606,7 +641,7 @@
     bufs, sems = rest[:5], rest[5:]
     a = along_steps(src, out, sems[7:], lax.axis_index("row") < NP)
     r = reduce_steps(1, None, part, rest_out, bufs, sems[:7])
-    drive((a, 1), (r, 1), (a, 3), (r, 1), (a, 3), (r, 1), (a, 1), (r, 1), (a, 3), (a, 1), (r, 1))
+    drive((r, 1), (a, 3), (r, 1), (a, 3), (r, 1), (a, 2), (r, 1), (a, 1), (r, 1), (a, 3), (r, 1))
 
 
 def along_reduce(half, part):

time: 299 us -> 290 us (0.970)
  Pallas kernels: 278 us -> 269 us
    pallas_call x1, Pallas kernels: 52 us -> 43.4 us  [along_reduce(): pl.pallas_call(along_reduce_kernel, out_shape=(jax.ShapeDtypeStruct((2, 2...]
where the time goes in v4:
time: 290 us
  Pallas kernels  269 us (93%)
  matrix products  11.6 us (4%)
  local copies, waits for them, and re-layouts  6.18 us (2%)
    pallas_call x1, Pallas kernels, along_spread(): pl.pallas_call(along_spread_kernel, out_shape=(jax.ShapeDtypeStruct((2, 2...  51.8 us
    pallas_call x1, Pallas kernels, spread(): pl.pallas_call(spread_kernel, out_shape=(jax.ShapeDtypeStruct((3, 4, 4, 3...  50.8 us
    pallas_call x1, Pallas kernels, reduce_rows(): pl.pallas_call(reduce_kernel, out_shape=jax.ShapeDtypeStruct((2, 3, 4, 4,...  48 us
    pallas_call x1, Pallas kernels, chain(): pl.pallas_call(chain_kernel, out_shape=(jax.ShapeDtypeStruct((256, 3 * NB...  46.2 us
    pallas_call x1, Pallas kernels, along_reduce(): pl.pallas_call(along_reduce_kernel, out_shape=(jax.ShapeDtypeStruct((2, 2...  43.4 us
    pallas_call x1, Pallas kernels, finish(): pl.pallas_call(finish_kernel, out_shape=jax.ShapeDtypeStruct((NB, 2 * NB)...  14.7 us
    pallas_call x1, Pallas kernels, invert(): pl.pallas_call(invert_kernel, out_shape=jax.ShapeDtypeStruct((NP, NB, NB)...  14.4 us
    dot_general x1, matrix products, dot_t(): lax.dot_general(a, b, (((0,), (0,)), ((), ())), precision=precision, pref...  7.74 us

profile of v4, /device:TPU:1, one launch (start us, length us, event | category | flops | bytes accessed | tf_op | source)
XLA Modules:
  0.0 289.9 jit_solution(1292757680802069423)
XLA Ops:
  0.0 50.8 %shard_map.46 = (f32[3,4,4,32,1024]{4,3,2,1,0:T(8,128)}, f32[2,3,4,4,32,512]{5,4,3,2,1,0:T(8,128)}, f32[256,1024]{1,0:T(8,128)}) custom-call(f32[4,4,32,1024]{3,2,1,0:T(8,128)} %bitcast.61, f32[512,1024]{1,0:T(8,128)} %cot.3), custom_call_target="tpu_custom_call" | custom-call | tf_op jit(solution)/shard_map/pallas_call | solution.py:564
  50.8 0.2 dynamic-slice_select_fusion
  51.0 2.2 slice_bitcast_fusion.14
  53.2 0.0 slice-start
  53.2 0.3 pad_maximum_fusion.d_ref
  53.5 0.0 slice-start.1
  53.5 14.4 %shard_map.47.i_ref = f32[3,512,512]{2,1,0:T(8,128)S(1)} custom-call(f32[3,512,512]{2,1,0:T(8,128)S(1)} %pad_maximum_fusion.d_ref), custom_call_target="tpu_custom_call" | custom-call | tf_op jit(solution)/shard_map/pallas_call | solution.py:703
  67.9 0.6 fusion.2
  68.6 0.7 convolution_subtract_fusion.2
  69.3 0.7 convolution_subtract_fusion.1
  69.9 0.6 fusion.1
  70.6 0.6 convolution_subtract_fusion
  71.2 0.6 fusion
  71.8 1.3 pad_maximum_fusion.1
  73.1 51.8 %shard_map.48 = (f32[2,2,8,16,1536]{4,3,2,1,0:T(8,128)}, f32[3,4,4,32,1024]{4,3,2,1,0:T(8,128)}) custom-call(f32[1,2,8,16,1536]{4,3,2,1,0:T(8,128)} %bitcast.63, f32[4,4,32,1024]{3,2,1,0:T(8,128)} %bitcast.62, f32[3,4,4,32,1024]{4,3,2,1,0:T(8,128)} %get-tuple-element.16._), custom_call_target="tpu_custom_call", output_to_operand_aliasing={{1}: (2, {})} | custom-call | tf_op jit(solution)/shard_map/pallas_call | solution.py:592
  124.9 7.7 %negate_select_fusion = f32[1536,1024]{1,0:T(8,128)S(1)} fusion(f32[512,1536]{1,0:T(8,128)} %bitcast.47, f32[512,1024]{1,0:T(8,128)} %param.4, pred[]{:T(512)S(6)} %ge.3), kind=kOutput, calls=%fused_computation | convolution fusion | flops 4834983936 | bytes 11534337 | tf_op jit(solution)/shard_map/dot_general | solution.py:21
  132.6 1.0 broadcast_select_fusion.src.part
  133.7 48.0 %shard_map.49 = f32[2,3,4,4,32,512]{5,4,3,2,1,0:T(8,128)S(1)} custom-call(f32[3,4,4,32,1024]{4,3,2,1,0:T(8,128)S(1)} %broadcast_select_fusion.src.part), custom_call_target="tpu_custom_call" | custom-call | tf_op jit(solution)/shard_map/pallas_call | solution.py:629
  181.6 0.0 copy-start
  181.6 2.6 copy-done
  184.2 46.2 %shard_map.50 = (f32[256,1536]{1,0:T(8,128)}, f32[3,512,512]{2,1,0:T(8,128)}) custom-call(s32[41,6]{1,0:T(8,128)} %constant.35.clone.plan_ref, s32[3,6]{1,0:T(4,128)} %constant.36.clone.pick_ref, f32[6,512,512]{2,1,0:T(8,128)} %bitcast.54, f32[6,512,512]{2,1,0:T(8,128)} %bitcast.44, f32[3,512,512]{2,1,0:T(8,128)} %copy-done.2), custom_call_target="tpu_custom_call" | custom-call | tf_op jit(solution)/shard_map/pallas_call | solution.py:833
  230.4 1.4 copy-done.4
  231.8 43.4 %shard_map.51 = (f32[2,2,8,16,1536]{4,3,2,1,0:T(8,128)S(1)}, f32[3,4,4,32,512]{4,3,2,1,0:T(8,128)S(1)}) custom-call(f32[1,2,8,16,1536]{4,3,2,1,0:T(8,128)S(1)} %bitcast.51, f32[3,4,4,32,1024]{4,3,2,1,0:T(8,128)S(1)} %broadcast_select_fusion.src.part), custom_call_target="tpu_custom_call" | custom-call | tf_op jit(solution)/shard_map/pallas_call | solution.py:648
  275.2 14.7 %shard_map.52 = f32[512,1024]{1,0:T(8,128)} custom-call(f32[512,1024]{1,0:T(8,128)S(1)} %copy-done.1, f32[512,1536]{1,0:T(8,128)S(1)} %bitcast.48, f32[512,1536]{1,0:T(8,128)S(1)} %bitcast.49, f32[1536,1024]{1,0:T(8,128)} %bitcast.60, f32[3,512,512]{2,1,0:T(8,128)S(1)} %bitcast.50, f32[2,3,512,512]{3,2,1,0:T(8,128)} %bitcast.45, ...), custom_call_target="tpu_custom_call" | custom-call | tf_op jit(solution)/shard_map/pallas_call | solution.py:936
  (13 shorter events, 0.0 us)
Async XLA Ops:
  0.0 50.8 %copy-start.1 = (f32[512,1024]{1,0:T(8,128)S(1)}, f32[512,1024]{1,0:T(8,128)}, u32[]{:S(2)}) copy-start(f32[512,1024]{1,0:T(8,128)} %cot.3) | copy-start | bytes 6291460
  53.2 15.4 %slice-start = ((s8[6291456]{0:T(1024)(128)(4,1)}), s8[4194304]{0:T(1024)(128)(4,1)S(1)}, s32[]{:S(2)}) async-start(s8[6291456]{0:T(1024)(128)(4,1)} %bitcast.55), calls=%async_computation | async-start | bytes 8388608
  53.5 15.1 %slice-start.1 = ((s8[6291456]{0:T(1024)(128)(4,1)}), s8[2097152]{0:T(1024)(128)(4,1)S(1)}, s32[]{:S(2)}) async-start(s8[6291456]{0:T(1024)(128)(4,1)} %bitcast.55), calls=%async_computation.1 | async-start | bytes 4194304
  53.5 15.1 %copy-start.5 = (f32[256,1024]{1,0:T(8,128)S(1)}, f32[256,1024]{1,0:T(8,128)}, u32[]{:S(2)}) copy-start(f32[256,1024]{1,0:T(8,128)} %get-tuple-element.14) | copy-start | bytes 3145732
  67.9 3.3 %copy-start.2 = (f32[3,512,512]{2,1,0:T(8,128)}, f32[3,512,512]{2,1,0:T(8,128)S(1)}, u32[]{:S(2)}) copy-start(f32[3,512,512]{2,1,0:T(8,128)S(1)} %shard_map.47.i_ref) | copy-start | bytes 9437188
  181.6 2.6 copy-start
  230.4 1.4 copy-start.4
  231.8 43.4 %copy-start.3 = (f32[2,2,8,16,1536]{4,3,2,1,0:T(8,128)S(1)}, f32[2,2,8,16,1536]{4,3,2,1,0:T(8,128)}, u32[]{:S(2)}) copy-start(f32[2,2,8,16,1536]{4,3,2,1,0:T(8,128)} %get-tuple-element.17) | copy-start | bytes 9437188

commit v5 on v4

--- a/solution.py
+++ b/solution.py
@@ -585,7 +585,7 @@
     greet(with_z(*place()))
     a = along_steps(src, out, sems[7:], lax.axis_index("row") >= NP)
     s = spread_steps(1, own, strips, sems[:7])
-    drive((s, 1), (a, 1), (a, 2), (s, 1), (a, 2), (s, 1), (a, 4), (s, 1), (a, 2), (a, 1), (s, 3))
+    drive((s, 1), (a, 5), (s, 1), (a, 2), (s, 1), (a, 3), (s, 1), (a, 1), (s, 1), (a, 1), (s, 2))
 
 
 def along_spread(half, factor, strips):

time: 290 us -> 290 us (level)
  no operation moved by 1% of the time
where the time goes in v5:
time: 290 us; the launch traced here: 289 us
  Pallas kernels  269 us (93%)
  matrix products  11.5 us (4%)
  local copies, waits for them, and re-layouts  6.18 us (2%)
    pallas_call x1, Pallas kernels, spread(): pl.pallas_call(spread_kernel, out_shape=(jax.ShapeDtypeStruct((3, 4, 4, 3...  50.8 us
    pallas_call x1, Pallas kernels, reduce_rows(): pl.pallas_call(reduce_kernel, out_shape=jax.ShapeDtypeStruct((2, 3, 4, 4,...  50 us
    pallas_call x1, Pallas kernels, along_spread(): pl.pallas_call(along_spread_kernel, out_shape=(jax.ShapeDtypeStruct((2, 2...  49.8 us
    pallas_call x1, Pallas kernels, chain(): pl.pallas_call(chain_kernel, out_shape=(jax.ShapeDtypeStruct((256, 3 * NB...  46.2 us
    pallas_call x1, Pallas kernels, along_reduce(): pl.pallas_call(along_reduce_kernel, out_shape=(jax.ShapeDtypeStruct((2, 2...  42.9 us
    pallas_call x1, Pallas kernels, finish(): pl.pallas_call(finish_kernel, out_shape=jax.ShapeDtypeStruct((NB, 2 * NB)...  14.7 us
    pallas_call x1, Pallas kernels, invert(): pl.pallas_call(invert_kernel, out_shape=jax.ShapeDtypeStruct((NP, NB, NB)...  14.4 us
    dot_general x1, matrix products, dot_t(): lax.dot_general(a, b, (((0,), (0,)), ((), ())), precision=precision, pref...  7.74 us

profile of v5, /device:TPU:1, one launch (start us, length us, event | category | flops | bytes accessed | tf_op | source)
XLA Modules:
  0.0 289.4 jit_solution(15533857206809022433)
XLA Ops:
  0.0 50.8 %shard_map.46 = (f32[3,4,4,32,1024]{4,3,2,1,0:T(8,128)}, f32[2,3,4,4,32,512]{5,4,3,2,1,0:T(8,128)}, f32[256,1024]{1,0:T(8,128)}) custom-call(f32[4,4,32,1024]{3,2,1,0:T(8,128)} %bitcast.61, f32[512,1024]{1,0:T(8,128)} %cot.3), custom_call_target="tpu_custom_call" | custom-call | tf_op jit(solution)/shard_map/pallas_call | solution.py:564
  50.8 0.2 dynamic-slice_select_fusion
  51.0 2.2 slice_bitcast_fusion.14
  53.2 0.0 slice-start
  53.2 0.3 pad_maximum_fusion.d_ref
  53.5 0.0 slice-start.1
  53.5 14.4 %shard_map.47.i_ref = f32[3,512,512]{2,1,0:T(8,128)S(1)} custom-call(f32[3,512,512]{2,1,0:T(8,128)S(1)} %pad_maximum_fusion.d_ref), custom_call_target="tpu_custom_call" | custom-call | tf_op jit(solution)/shard_map/pallas_call | solution.py:703
  67.9 0.6 fusion.2
  68.6 0.7 convolution_subtract_fusion.2
  69.3 0.7 convolution_subtract_fusion.1
  69.9 0.6 fusion.1
  70.6 0.6 convolution_subtract_fusion
  71.2 0.6 fusion
  71.8 1.3 pad_maximum_fusion.1
  73.1 49.8 %shard_map.48 = (f32[2,2,8,16,1536]{4,3,2,1,0:T(8,128)}, f32[3,4,4,32,1024]{4,3,2,1,0:T(8,128)}) custom-call(f32[1,2,8,16,1536]{4,3,2,1,0:T(8,128)} %bitcast.63, f32[4,4,32,1024]{3,2,1,0:T(8,128)} %bitcast.62, f32[3,4,4,32,1024]{4,3,2,1,0:T(8,128)} %get-tuple-element.16._), custom_call_target="tpu_custom_call", output_to_operand_aliasing={{1}: (2, {})} | custom-call | tf_op jit(solution)/shard_map/pallas_call | solution.py:592
  122.9 7.7 %negate_select_fusion = f32[1536,1024]{1,0:T(8,128)S(1)} fusion(f32[512,1536]{1,0:T(8,128)} %bitcast.47, f32[512,1024]{1,0:T(8,128)} %param.4, pred[]{:T(512)S(6)} %ge.3), kind=kOutput, calls=%fused_computation | convolution fusion | flops 4834983936 | bytes 11534337 | tf_op jit(solution)/shard_map/dot_general | solution.py:21
  130.6 1.0 broadcast_select_fusion.src.part
  131.7 50.0 %shard_map.49 = f32[2,3,4,4,32,512]{5,4,3,2,1,0:T(8,128)S(1)} custom-call(f32[3,4,4,32,1024]{4,3,2,1,0:T(8,128)S(1)} %broadcast_select_fusion.src.part), custom_call_target="tpu_custom_call" | custom-call | tf_op jit(solution)/shard_map/pallas_call | solution.py:629
  181.7 0.0 copy-start
  181.7 2.6 copy-done
  184.3 46.2 %shard_map.50 = (f32[256,1536]{1,0:T(8,128)}, f32[3,512,512]{2,1,0:T(8,128)}) custom-call(s32[41,6]{1,0:T(8,128)} %constant.35.clone.plan_ref, s32[3,6]{1,0:T(4,128)} %constant.36.clone.pick_ref, f32[6,512,512]{2,1,0:T(8,128)} %bitcast.54, f32[6,512,512]{2,1,0:T(8,128)} %bitcast.44, f32[3,512,512]{2,1,0:T(8,128)} %copy-done.2), custom_call_target="tpu_custom_call" | custom-call | tf_op jit(solution)/shard_map/pallas_call | solution.py:833
  230.4 1.4 copy-done.4
  231.8 42.9 %shard_map.51 = (f32[2,2,8,16,1536]{4,3,2,1,0:T(8,128)S(1)}, f32[3,4,4,32,512]{4,3,2,1,0:T(8,128)S(1)}) custom-call(f32[1,2,8,16,1536]{4,3,2,1,0:T(8,128)S(1)} %bitcast.51, f32[3,4,4,32,1024]{4,3,2,1,0:T(8,128)S(1)} %broadcast_select_fusion.src.part), custom_call_target="tpu_custom_call" | custom-call | tf_op jit(solution)/shard_map/pallas_call | solution.py:648
  274.8 14.7 %shard_map.52 = f32[512,1024]{1,0:T(8,128)} custom-call(f32[512,1024]{1,0:T(8,128)S(1)} %copy-done.1, f32[512,1536]{1,0:T(8,128)S(1)} %bitcast.48, f32[512,1536]{1,0:T(8,128)S(1)} %bitcast.49, f32[1536,1024]{1,0:T(8,128)} %bitcast.60, f32[3,512,512]{2,1,0:T(8,128)S(1)} %bitcast.50, f32[2,3,512,512]{3,2,1,0:T(8,128)} %bitcast.45, ...), custom_call_target="tpu_custom_call" | custom-call | tf_op jit(solution)/shard_map/pallas_call | solution.py:936
  (13 shorter events, 0.0 us)
Async XLA Ops:
  0.0 50.8 %copy-start.1 = (f32[512,1024]{1,0:T(8,128)S(1)}, f32[512,1024]{1,0:T(8,128)}, u32[]{:S(2)}) copy-start(f32[512,1024]{1,0:T(8,128)} %cot.3) | copy-start | bytes 6291460
  53.2 15.4 %slice-start = ((s8[6291456]{0:T(1024)(128)(4,1)}), s8[4194304]{0:T(1024)(128)(4,1)S(1)}, s32[]{:S(2)}) async-start(s8[6291456]{0:T(1024)(128)(4,1)} %bitcast.55), calls=%async_computation | async-start | bytes 8388608
  53.5 15.1 %slice-start.1 = ((s8[6291456]{0:T(1024)(128)(4,1)}), s8[2097152]{0:T(1024)(128)(4,1)S(1)}, s32[]{:S(2)}) async-start(s8[6291456]{0:T(1024)(128)(4,1)} %bitcast.55), calls=%async_computation.1 | async-start | bytes 4194304
  53.5 15.1 %copy-start.5 = (f32[256,1024]{1,0:T(8,128)S(1)}, f32[256,1024]{1,0:T(8,128)}, u32[]{:S(2)}) copy-start(f32[256,1024]{1,0:T(8,128)} %get-tuple-element.14) | copy-start | bytes 3145732
  67.9 3.3 %copy-start.2 = (f32[3,512,512]{2,1,0:T(8,128)}, f32[3,512,512]{2,1,0:T(8,128)S(1)}, u32[]{:S(2)}) copy-start(f32[3,512,512]{2,1,0:T(8,128)S(1)} %shard_map.47.i_ref) | copy-start | bytes 9437188
  181.7 2.6 copy-start
  230.4 1.4 copy-start.4
  231.8 42.9 %copy-start.3 = (f32[2,2,8,16,1536]{4,3,2,1,0:T(8,128)S(1)}, f32[2,2,8,16,1536]{4,3,2,1,0:T(8,128)}, u32[]{:S(2)}) copy-start(f32[2,2,8,16,1536]{4,3,2,1,0:T(8,128)} %get-tuple-element.17) | copy-start | bytes 9437188

commit v6 on v5

--- a/solution.py
+++ b/solution.py
@@ -571,7 +571,7 @@
         in_specs=[ANY, ANY],
         out_specs=(ANY, VM, VM),
         scratch_shapes=SPREAD_SEMS + [DMA((2, 3, 4))] * 3 + [DMA((1,)), DMA((1,))],
-        compiler_params=comm(0, 60),
+        compiler_params=comm(0, 32),
     )(factor.reshape(4, 4, 32, 1024), cot)
 
 
@@ -599,7 +599,7 @@
         out_specs=(VM, ANY),
         scratch_shapes=SPREAD_SEMS + ALONG_SEMS,
         input_output_aliases={2: 1},
-        compiler_params=comm(1, 60),
+        compiler_params=comm(1, 16),
     )(half.reshape(1, 2, CH, CR, 1536), factor.reshape(4, 4, 32, 1024), strips)
     return out.reshape(512, 1536), strips.reshape(1536, 1024)
 

time: 290 us -> 279 us (0.962)
  Pallas kernels: 269 us -> 260 us
    pallas_call x1, Pallas kernels: 50.8 us -> 46.6 us  [spread(): pl.pallas_call(spread_kernel, out_shape=(jax.ShapeDtypeStruct((3, 4, 4, 3...]
    pallas_call x1, Pallas kernels: 49.8 us -> 45.9 us  [along_spread(): pl.pallas_call(along_spread_kernel, out_shape=(jax.ShapeDtypeStruct((2, 2...]
    unnamed x16 -> x20, local copies, waits for them, and re-layouts: 4.01 us -> 7.19 us
where the time goes in v6:
time: 279 us
  Pallas kernels  260 us (93%)
  matrix products  8.89 us (3%)
  local copies, waits for them, and re-layouts  7.51 us (3%)
    pallas_call x1, Pallas kernels, reduce_rows(): pl.pallas_call(reduce_kernel, out_shape=jax.ShapeDtypeStruct((2, 3, 4, 4,...  49.3 us
    pallas_call x1, Pallas kernels, spread(): pl.pallas_call(spread_kernel, out_shape=(jax.ShapeDtypeStruct((3, 4, 4, 3...  46.6 us
    pallas_call x1, Pallas kernels, chain(): pl.pallas_call(chain_kernel, out_shape=(jax.ShapeDtypeStruct((256, 3 * NB...  46.1 us
    pallas_call x1, Pallas kernels, along_spread(): pl.pallas_call(along_spread_kernel, out_shape=(jax.ShapeDtypeStruct((2, 2...  45.9 us
    pallas_call x1, Pallas kernels, along_reduce(): pl.pallas_call(along_reduce_kernel, out_shape=(jax.ShapeDtypeStruct((2, 2...  43.5 us
    pallas_call x1, Pallas kernels, finish(): pl.pallas_call(finish_kernel, out_shape=jax.ShapeDtypeStruct((NB, 2 * NB)...  14.7 us
    pallas_call x1, Pallas kernels, invert(): pl.pallas_call(invert_kernel, out_shape=jax.ShapeDtypeStruct((NP, NB, NB)...  14.3 us
    unnamed x20, local copies, waits for them, and re-layouts  7.19 us

profile of v6, /device:TPU:1, one launch (start us, length us, event | category | flops | bytes accessed | tf_op | source)
XLA Modules:
  0.0 279.3 jit_solution(10513276570424328310)
XLA Ops:
  0.0 1.6 copy-done.1
  1.6 1.6 copy-done.8
  3.2 46.6 %shard_map.46 = (f32[3,4,4,32,1024]{4,3,2,1,0:T(8,128)S(1)}, f32[2,3,4,4,32,512]{5,4,3,2,1,0:T(8,128)S(1)}, f32[256,1024]{1,0:T(8,128)S(1)}) custom-call(f32[4,4,32,1024]{3,2,1,0:T(8,128)S(1)} %bitcast.55, f32[512,1024]{1,0:T(8,128)S(1)} %copy-done.1), custom_call_target="tpu_custom_call" | custom-call | tf_op jit(solution)/shard_map/pallas_call | solution.py:564
  49.8 0.2 dynamic-slice_select_fusion
  50.0 0.3 slice_bitcast_fusion.14
  50.3 0.3 pad_maximum_fusion.d_ref
  50.6 14.3 %shard_map.47.i_ref = f32[3,512,512]{2,1,0:T(8,128)S(1)} custom-call(f32[3,512,512]{2,1,0:T(8,128)S(1)} %pad_maximum_fusion.d_ref), custom_call_target="tpu_custom_call" | custom-call | tf_op jit(solution)/shard_map/pallas_call | solution.py:703
  65.0 0.6 fusion.2
  65.6 0.6 convolution_subtract_fusion.2
  66.2 0.6 convolution_subtract_fusion.1
  66.8 0.6 fusion.1
  67.5 0.6 convolution_subtract_fusion
  68.1 0.6 fusion
  68.7 0.1 pad_maximum_fusion.1
  68.8 45.9 %shard_map.48 = (f32[2,2,8,16,1536]{4,3,2,1,0:T(8,128)S(1)}, f32[3,4,4,32,1024]{4,3,2,1,0:T(8,128)S(1)}) custom-call(f32[1,2,8,16,1536]{4,3,2,1,0:T(8,128)S(1)} %bitcast.57, f32[4,4,32,1024]{3,2,1,0:T(8,128)S(1)} %bitcast.56, f32[3,4,4,32,1024]{4,3,2,1,0:T(8,128)S(1)} %get-tuple-element.16._), custom_call_target="tpu_custom_call", output_to_operand_aliasing={{1}: (2, {})} | custom-call | tf_op jit(solution)/shard_map/pallas_call | solution.py:592
  114.7 0.0 copy-start.2
  114.7 5.2 %negate_select_fusion = f32[1536,1024]{1,0:T(8,128)S(1)} fusion(f32[512,1536]{1,0:T(8,128)S(1)} %bitcast.53, f32[512,1024]{1,0:T(8,128)S(1)} %copy-done.8, pred[]{:T(512)S(6)} %ge.3), kind=kOutput, calls=%fused_computation | convolution fusion | flops 4834983936 | bytes 11534337 | tf_op jit(solution)/shard_map/dot_general | solution.py:21
  120.0 1.7 broadcast_select_fusion.src.part
  121.7 49.3 %shard_map.49 = f32[2,3,4,4,32,512]{5,4,3,2,1,0:T(8,128)S(1)} custom-call(f32[3,4,4,32,1024]{4,3,2,1,0:T(8,128)S(1)} %broadcast_select_fusion.src.part), custom_call_target="tpu_custom_call" | custom-call | tf_op jit(solution)/shard_map/pallas_call | solution.py:629
  171.0 2.6 copy-done
  173.6 46.1 %shard_map.50 = (f32[256,1536]{1,0:T(8,128)}, f32[3,512,512]{2,1,0:T(8,128)}) custom-call(s32[41,6]{1,0:T(8,128)} %constant.35.clone.plan_ref, s32[3,6]{1,0:T(4,128)} %constant.36.clone.pick_ref, f32[6,512,512]{2,1,0:T(8,128)} %bitcast.51, f32[6,512,512]{2,1,0:T(8,128)} %bitcast.44, f32[3,512,512]{2,1,0:T(8,128)} %copy-done.3), custom_call_target="tpu_custom_call" | custom-call | tf_op jit(solution)/shard_map/pallas_call | solution.py:833
  219.7 1.4 copy-done.9
  221.1 43.5 %shard_map.51 = (f32[2,2,8,16,1536]{4,3,2,1,0:T(8,128)S(1)}, f32[3,4,4,32,512]{4,3,2,1,0:T(8,128)S(1)}) custom-call(f32[1,2,8,16,1536]{4,3,2,1,0:T(8,128)S(1)} %bitcast.60, f32[3,4,4,32,1024]{4,3,2,1,0:T(8,128)S(1)} %broadcast_select_fusion.src.part), custom_call_target="tpu_custom_call" | custom-call | tf_op jit(solution)/shard_map/pallas_call | solution.py:648
  264.6 14.7 %shard_map.52 = f32[512,1024]{1,0:T(8,128)} custom-call(f32[512,1024]{1,0:T(8,128)S(1)} %copy-done.2, f32[512,1536]{1,0:T(8,128)S(1)} %bitcast.54, f32[512,1536]{1,0:T(8,128)S(1)} %bitcast.58, f32[1536,1024]{1,0:T(8,128)} %bitcast.52, f32[3,512,512]{2,1,0:T(8,128)S(1)} %bitcast.59, f32[2,3,512,512]{3,2,1,0:T(8,128)} %bitcast.45, ...), custom_call_target="tpu_custom_call" | custom-call | tf_op jit(solution)/shard_map/pallas_call | solution.py:936
  (16 shorter events, 0.0 us)
Async XLA Ops:
  0.0 1.6 copy-start.1
  1.6 1.6 copy-start.8
  49.8 17.7 %copy-start.4 = (f32[2,3,4,4,32,512]{5,4,3,2,1,0:T(8,128)}, f32[2,3,4,4,32,512]{5,4,3,2,1,0:T(8,128)S(1)}, u32[]{:S(2)}) copy-start(f32[2,3,4,4,32,512]{5,4,3,2,1,0:T(8,128)S(1)} %get-tuple-element.15) | copy-start | bytes 18874372
  64.9 3.1 %copy-start.3 = (f32[3,512,512]{2,1,0:T(8,128)}, f32[3,512,512]{2,1,0:T(8,128)S(1)}, u32[]{:S(2)}) copy-start(f32[3,512,512]{2,1,0:T(8,128)S(1)} %shard_map.47.i_ref) | copy-start | bytes 9437188
  114.7 5.2 %copy-start.5 = (f32[3,4,4,32,1024]{4,3,2,1,0:T(8,128)}, f32[3,4,4,32,1024]{4,3,2,1,0:T(8,128)S(1)}, u32[]{:S(2)}) copy-start(f32[3,4,4,32,1024]{4,3,2,1,0:T(8,128)S(1)} %get-tuple-element.20) | copy-start | bytes 18874372
  114.7 5.2 %copy-start.6 = (f32[2,2,8,16,1536]{4,3,2,1,0:T(8,128)}, f32[2,2,8,16,1536]{4,3,2,1,0:T(8,128)S(1)}, u32[]{:S(2)}) copy-start(f32[2,2,8,16,1536]{4,3,2,1,0:T(8,128)S(1)} %get-tuple-element.17) | copy-start | bytes 9437188
  114.7 5.2 %copy-start.2 = (f32[512,1024]{1,0:T(8,128)S(1)}, f32[512,1024]{1,0:T(8,128)}, u32[]{:S(2)}) copy-start(f32[512,1024]{1,0:T(8,128)} %cot.3) | copy-start | bytes 6291460
  171.0 2.6 copy-start
  219.7 1.4 copy-start.9
  221.1 43.5 %copy-start.7 = (f32[2,2,8,16,1536]{4,3,2,1,0:T(8,128)S(1)}, f32[2,2,8,16,1536]{4,3,2,1,0:T(8,128)}, u32[]{:S(2)}) copy-start(f32[2,2,8,16,1536]{4,3,2,1,0:T(8,128)} %copy-done.6) | copy-start | bytes 9437188
